TPU v7x, 1024 devices: a whole 4x8x16 slice. The times are simulated.
1024 devices in a mesh: wave: 16 (over y, core), sect: 64 (over x, z).
Axes of the slice: x: 4, y: 8, z: 16, core: 2. Of those that a mesh axis runs over, the one named last changes fastest.
Arguments:
- spec_in: bfloat16 [32, 2, 64, 640], P('wave', None, 'sect'), may hold values from -6 to 6
- pair_low: int32 [32], replicated, may hold values from 1 to 319, as said below
- row_points: int32 [640], replicated, may hold values from 20 to 2576, as said below
- legendre: bfloat16 [32, 640, 640], P('wave'), as said below
- gauss_weight: float32 [640], replicated, may hold values from 0 to 1, as said below
- couple: bfloat16 [64, 64], replicated, may hold values from -0.75 to 0.75
- point_factor: float32 [2, 64, 26240], P(None, 'sect', 'wave'), may hold values from 0.25 to 4
Outputs:
- grid_field: bfloat16 [2, 64, 64, 26240], P(None, None, 'sect', 'wave')
- spec_out: float32 [32, 2, 64, 640], P('wave', None, 'sect')
Inputs may be any that keep to these rules, and one draw needn't show every extreme that they name: `pair_low`: the lower wavenumbers are distinct; 1 and 319 are always among them, the others are drawn. row_points[j] = 20 + 4 i where i (0 to 639, counted from the pole) is the row pair at position j; every row pair appears once; the block of 40 positions of one band holds row pairs from every latitude. legendre[p, s, j] is the associated Legendre function of slot s of pair p (slot_wave), normalized to unit integral of its square over -1 to 1, at the northern latitude of the row pair at position j; the southern row has the parity sign. `gauss_weight`: the quadrature weight of the latitude of the row pair at position j, the same for its northern and southern row.
All inputs are finite; a program needn't handle non-finite values.
Results may differ from a plain program's by a relative error of at most 0.0062.
Values may be sent and summed in bfloat16 or wider, within the bound.
No kernel may reach another device: no remote copies, remote signals or barrier semaphores. Data moves between devices by JAX's collectives and lax.ppermute only.
A program may use at most 32 MiB of HBM per device.

v0:
```python
import math

import jax
import jax.numpy as jnp
from jax import lax
from jax.sharding import Mesh
from jax.sharding import PartitionSpec as P

WAVE = ("wave_0", "wave_1")


def in_blocks(x, dim, size):
    before, after = (x.shape[:dim], x.shape[dim + 1 :])
    return jnp.moveaxis(x.reshape(*before, size, -1, *after), dim, 0)


def in_order(parts, dim):
    parts = jnp.moveaxis(parts, 0, dim)
    shape = parts.shape
    return parts.reshape(*shape[:dim], shape[dim] * shape[dim + 1], *shape[dim + 2 :])


def exchange_in_order(parts, axes, turns):
    shape = [lax.axis_size(a) for a in axes]
    parts = parts.reshape(*shape, *parts.shape[1:])
    for k in turns:
        parts = lax.all_to_all(parts, axes[k], split_axis=k, concat_axis=k, tiled=True)
    return parts.reshape(-1, *parts.shape[len(axes) :])


def exchange_by_axis(x, axes, turns, split_dim, concat_dim):
    parts = in_blocks(x, split_dim, lax.axis_size(axes))
    return in_order(exchange_in_order(parts, axes, turns), concat_dim)


def slot_tables(pair_low, slot_count):
    slot_index = jnp.arange(slot_count, dtype=jnp.int32)
    lower_wave = pair_low[:, None]
    leading = slot_index[None, :] < slot_count - lower_wave
    order_of = jnp.where(leading, lower_wave, slot_count - lower_wave)
    degree = jnp.where(leading, lower_wave + slot_index[None, :], slot_index[None, :])
    odd_parity = (degree + order_of) % 2 == 1
    return (leading, odd_parity)


def spread_spectral(spec_in, leading, odd_parity):
    parity_sign = jnp.where(odd_parity, -1.0, 1.0).astype(jnp.float32)
    member_mask = jnp.stack([leading, jnp.logical_not(leading)], axis=1).astype(jnp.float32)
    hemisphere = jnp.stack([jnp.ones_like(parity_sign), parity_sign], axis=1)
    slot_factor = (member_mask[:, :, None, :] * hemisphere[:, None, :, :]).astype(jnp.bfloat16)
    return spec_in[:, None, None, :, :, :] * slot_factor[:, :, :, None, None, :]


def sector_phases(wave_list, band_points, sector_width, sectors, columns):
    sector_start = sectors[None, :] * sector_width[:, None]
    outer_index = wave_list[None, None, :] * sector_start[:, :, None] % band_points[:, None, None]
    outer_angle = (
        2.0
        * math.pi
        * outer_index.astype(jnp.float32)
        / band_points.astype(jnp.float32)[:, None, None]
    )
    inside = columns[None, None, :] < sector_width[:, None, None]
    valid_mask = inside & (
        sector_start[:, :, None] + columns[None, None, :] < band_points[:, None, None]
    )
    return (jnp.cos(outer_angle), jnp.sin(outer_angle), valid_mask)


def rotate_coeffs(fourier, cos_outer, sin_outer, synth_scale):
    real_part = jnp.transpose(fourier[:, :, 0].astype(jnp.float32), (3, 1, 2, 0))[:, :, None]
    imag_part = jnp.transpose(fourier[:, :, 1].astype(jnp.float32), (3, 1, 2, 0))[:, :, None]
    cos_wide = cos_outer[:, None, :, None, :]
    sin_wide = sin_outer[:, None, :, None, :]
    rot_cos = synth_scale * (real_part * cos_wide - imag_part * sin_wide)
    rot_sin = synth_scale * (real_part * sin_wide + imag_part * cos_wide)
    return jnp.concatenate([rot_cos, rot_sin], axis=4).astype(jnp.bfloat16)


def synth_tile(rotated, trig_table, valid_mask):
    grid_tile = jnp.einsum(
        "rhnfq,rcq->rhnfc", rotated, trig_table, preferred_element_type=jnp.float32
    )
    grid_tile = jnp.where(valid_mask[:, None, :, None, :], grid_tile, 0.0).astype(jnp.bfloat16)
    return jnp.transpose(grid_tile, (1, 3, 2, 0, 4))


def fold_sectors(sector_sums, cos_outer, sin_outer, wave_total):
    cos_part = sector_sums[..., :wave_total]
    sin_part = sector_sums[..., wave_total:]
    cos_wide = cos_outer[:, None, :, None, :]
    sin_wide = sin_outer[:, None, :, None, :]
    real_sum = jnp.sum(cos_wide * cos_part + sin_wide * sin_part, axis=2)
    imag_sum = jnp.sum(cos_wide * sin_part - sin_wide * cos_part, axis=2)
    return jnp.transpose(jnp.stack([real_sum, imag_sum], axis=2), (3, 1, 2, 4, 0))


def per_device(spec_in, pair_low, row_points, legendre, gauss_weight, couple, point_factor):
    wave_count = lax.axis_size(WAVE)
    sect_count = lax.axis_size("sect")
    wave_rank = lax.axis_index(WAVE)
    pairs_dev = spec_in.shape[0]
    field_dev = spec_in.shape[2]
    slot_count = spec_in.shape[3]
    row_total = legendre.shape[2]
    pair_total = pairs_dev * wave_count
    band_rows = row_total // wave_count
    sector_cols = point_factor.shape[2] // band_rows
    wave_total = 2 * pair_total
    synth_scale = 2.0 / math.sqrt(2.0 * slot_count * pair_total)
    own_low = lax.dynamic_slice_in_dim(pair_low, wave_rank * pairs_dev, pairs_dev)
    leading, odd_parity = slot_tables(own_low, slot_count)
    spread_coeffs = spread_spectral(spec_in, leading, odd_parity).reshape(
        pairs_dev, 8 * field_dev, slot_count
    )
    fourier = jnp.einsum(
        "pks,psj->pkj", spread_coeffs, legendre, preferred_element_type=jnp.float32
    )
    fourier = fourier.reshape(pairs_dev, 2, 2, 2, field_dev, row_total)
    own_waves = jnp.stack([own_low, slot_count - own_low], axis=1)
    resolved = 2 * own_waves[:, :, None] < row_points[None, None, :]
    fourier = jnp.where(resolved[:, :, None, None, None, :], fourier, 0.0).astype(jnp.bfloat16)
    fourier = fourier.reshape(2 * pairs_dev, 2, 2, field_dev, row_total)
    banded = exchange_by_axis(fourier, WAVE, (1, 0), 4, 0)
    wave_list = jnp.stack([pair_low, slot_count - pair_low], axis=1).reshape(-1)
    band_points = lax.dynamic_slice_in_dim(row_points, wave_rank * band_rows, band_rows)
    sector_width = (band_points + sect_count - 1) // sect_count
    columns = jnp.arange(sector_cols, dtype=jnp.int32)
    inner_index = wave_list[None, None, :] * columns[None, :, None] % band_points[:, None, None]
    inner_angle = (
        2.0
        * math.pi
        * inner_index.astype(jnp.float32)
        / band_points.astype(jnp.float32)[:, None, None]
    )
    trig_table = jnp.concatenate([jnp.cos(inner_angle), -jnp.sin(inner_angle)], axis=2).astype(
        jnp.bfloat16
    )
    every_sector = jnp.arange(sect_count, dtype=jnp.int32)
    cos_every, sin_every, valid_every = sector_phases(
        wave_list, band_points, sector_width, every_sector, columns
    )
    rotated = rotate_coeffs(banded, cos_every, sin_every, synth_scale)
    local_grid = synth_tile(rotated, trig_table, valid_every).reshape(
        2, field_dev, sect_count, band_rows * sector_cols
    )
    grid_field = lax.all_to_all(local_grid, "sect", split_axis=2, concat_axis=1, tiled=True)
    coupled = jnp.einsum("hfux,fg->hgux", grid_field, couple, preferred_element_type=jnp.float32)
    tendency = (coupled * point_factor[:, None, :, :]).astype(jnp.bfloat16)
    cos_back, sin_back, valid_back = sector_phases(
        wave_list, band_points, sector_width, every_sector, columns
    )
    received = lax.all_to_all(tendency, "sect", split_axis=1, concat_axis=2, tiled=True)
    field_rows = received.reshape(2, field_dev, sect_count, band_rows, sector_cols)
    sector_sums = jnp.einsum(
        "hfnrc,rcq->rhnfq", field_rows, trig_table, preferred_element_type=jnp.float32
    )
    summed = fold_sectors(sector_sums, cos_back, sin_back, wave_total)
    inverse_scale = 2.0 / (synth_scale * band_points.astype(jnp.float32))
    keep_mask = 2 * wave_list[:, None] < band_points[None, :]
    analysis = jnp.where(keep_mask, summed * inverse_scale, 0.0).astype(jnp.bfloat16)
    returned = lax.all_to_all(analysis, WAVE, split_axis=3, concat_axis=4, tiled=True)
    returned = returned.astype(jnp.float32).reshape(field_dev, 2, 2, pairs_dev, 2, row_total)
    north_half = returned[:, 0]
    south_half = returned[:, 1]
    weighted = jnp.stack(
        [(north_half + south_half) * gauss_weight, (north_half - south_half) * gauss_weight], axis=0
    ).astype(jnp.bfloat16)
    weighted = jnp.transpose(weighted, (3, 4, 0, 2, 1, 5)).reshape(
        pairs_dev, 8 * field_dev, row_total
    )
    projected = jnp.einsum("pkj,psj->pks", weighted, legendre, preferred_element_type=jnp.float32)
    projected = projected.reshape(pairs_dev, 2, 2, 2, field_dev, slot_count)
    member_low = jnp.where(odd_parity[:, None, None, :], projected[:, 0, 1], projected[:, 0, 0])
    member_high = jnp.where(odd_parity[:, None, None, :], projected[:, 1, 1], projected[:, 1, 0])
    spec_out = jnp.where(leading[:, None, None, :], member_low, member_high)
    return (grid_field, spec_out)


def solution(mesh):
    split = Mesh(mesh.devices.reshape(8, 2, mesh.shape["sect"]), ("wave_0", "wave_1", "sect"))
    in_specs = (
        P(WAVE, None, "sect", None),
        P(),
        P(),
        P(WAVE, None, None),
        P(),
        P(),
        P(None, "sect", WAVE),
    )
    out_specs = (P(None, None, "sect", WAVE), P(WAVE, None, "sect", None))
    return jax.shard_map(
        per_device, mesh=split, in_specs=in_specs, out_specs=out_specs, check_vma=False
    )
```

profile of v0, /device:TPU:1, one launch (start us, length us, event | category | flops | bytes accessed | tf_op | source)
XLA Modules:
  0.0 175.6 jit_solution(17557052121229056629)
XLA Ops:
  0.7 0.8 fusion.35
  1.7 0.3 copy-done.9
  2.1 0.7 broadcast_multiply_fusion
  3.9 17.5 %all_to_all.40 = bf16[2,2,2560]{2,1,0:T(2,128)(2,1)S(1)} all-to-all(bf16[2,2,2560]{2,1,0:T(2,128)(2,1)S(1)} %reshape.664), channel_id=1, replica_groups=mesh['wave_0'=8,'wave_1'=2,'sect'=64] {'wave_1'}, dimensions={0} | all-to-all | bytes 40960 | tf_op jit(solution)/shard_map/all_to_all | solution.py:27
  21.6 0.7 reshape.666
  22.3 3.3 %all-to-all-start.1 = ((bf16[8,2,640]{2,1,0:T(2,128)(2,1)}), bf16[8,2,640]{2,1,0:T(2,128)(2,1)S(1)}, u32[]{:S(2)}, u32[]{:S(2)}) async-start(bf16[8,2,640]{2,1,0:T(2,128)(2,1)} %reshape.666), calls=%async_computation.1 | async-start | bytes 40960 | tf_op jit(solution)/shard_map/all_to_all | solution.py:27
  25.7 0.6 multiply_divide_fusion
  26.7 19.3 %fusion.22 = (f32[40,64,64]{2,1,0:T(8,128)S(1)}, f32[40,64,64]{2,1,0:T(8,128)}) fusion(f32[40]{0:T(128)S(1)} %get-tuple-element.32, pred[40]{0:T(512)(128)(4,1)S(1)} %compare_bitcast_fusion, s32[40]{0:T(128)S(1)} %fusion.32, s32[40,64]{1,0:T(8,128)S(1)} %iota_multiply_fusion.1, s32[64]{0:T(128)S(1)} %mul.315), kind=kLoop, calls=%fused_computation.38 | loop fusion | flops 1802240 | bytes 1321576 | tf_op jit(solution)/shard_map/cos | solution.py:67
  46.0 14.5 %cosine_convert_fusion = (bf16[40,41,64]{2,1,0:T(8,128)(2,1)S(1)}, bf16[40,41,64]{2,1,0:T(8,128)(2,1)}) fusion(f32[40]{0:T(128)S(1)} %get-tuple-element.32, pred[40]{0:T(512)(128)(4,1)S(1)} %broadcast_compare_fusion.2, s32[40]{0:T(128)S(1)} %get-tuple-element.31, s32[41,64]{1,0:T(8,128)S(1)} %iota_multiply_fusion), kind=kLoop, calls=%fused_computation.32 | loop fusion | flops 1364480 | bytes 430696 | tf_op jit(solution)/shard_map/convert.11
  60.5 1.2 fusion.18
  61.9 0.6 convert_bitcast_fusion.2
  62.6 0.9 copy.77
  63.5 0.7 copy.79
  64.2 2.3 %multiply_convert_fusion.1 = (bf16[40,2,64,64]{3,2,1,0:T(8,128)(2,1)S(1)}, bf16[40,2,64,64]{3,2,1,0:T(8,128)(2,1)S(1)}) fusion(f32[40,64,64]{2,1,0:T(8,128)} %get-tuple-element.28, f32[40,2,64]{2,1,0:T(2,128)} %copy.79, f32[40,64,64]{2,1,0:T(8,128)S(1)} %get-tuple-element.27, f32[40,2,64]{2,1,0:T(2,128)S(1)} %copy.77), kind=kLoop, calls=%fused_computation.3 | loop fusion | flops 3276800 | bytes 2662400 | tf_op jit(solution)/shard_map/convert.13
  66.5 1.4 fusion.3
  68.0 1.6 copy.80
  69.6 3.5 %copy.81 = bf16[2,1,64,1640]{3,0,1,2:T(2,128)(2,1)} copy(bf16[2,1,64,1640]{2,0,3,1:T(2,128)(2,1)} %bitcast.128) | data formatting | bytes 839680 | tf_op jit(solution)/shard_map/reshape | solution.py:144
  73.0 13.2 %all-to-all-start.2 = ((bf16[2,1,64,1640]{3,0,1,2:T(2,128)(2,1)}), bf16[2,1,64,1640]{3,0,1,2:T(2,128)(2,1)}, u32[]{:S(2)}, u32[]{:S(2)}) async-start(bf16[2,1,64,1640]{3,0,1,2:T(2,128)(2,1)} %copy.81), calls=%async_computation.2 | async-start | bytes 851968 | tf_op jit(solution)/shard_map/all_to_all | solution.py:147
  86.2 25.7 %all-to-all-done.2 = bf16[2,1,64,1640]{3,0,1,2:T(2,128)(2,1)} async-done(((bf16[2,1,64,1640]{3,0,1,2:T(2,128)(2,1)}), bf16[2,1,64,1640]{3,0,1,2:T(2,128)(2,1)}, u32[]{:S(2)}, u32[]{:S(2)}) %all-to-all-start.2) | async-done | bytes 419872 | tf_op jit(solution)/shard_map/all_to_all | solution.py:147
  112.0 1.3 fusion.2
  113.3 1.2 copy.84
  114.5 8.2 %all-to-all-start.3 = ((bf16[2,64,1,1640]{3,0,2,1:T(2,128)(2,1)}), bf16[2,64,1,1640]{3,0,2,1:T(2,128)(2,1)}, u32[]{:S(2)}, u32[]{:S(2)}) async-start(bf16[2,64,1,1640]{3,0,2,1:T(2,128)(2,1)} %copy.84), calls=%async_computation.3 | async-start | bytes 851968 | tf_op jit(solution)/shard_map/all_to_all | solution.py:153
  122.8 25.0 %all-to-all-done.3 = bf16[2,64,1,1640]{3,0,2,1:T(2,128)(2,1)} async-done(((bf16[2,64,1,1640]{3,0,2,1:T(2,128)(2,1)}), bf16[2,64,1,1640]{3,0,2,1:T(2,128)(2,1)}, u32[]{:S(2)}, u32[]{:S(2)}) %all-to-all-start.3) | async-done | bytes 419872 | tf_op jit(solution)/shard_map/all_to_all | solution.py:153
  147.8 3.5 %copy.85 = bf16[2,64,1,1640]{1,0,3,2:T(2,128)(2,1)} copy(bf16[2,64,1,1640]{3,0,2,1:T(2,128)(2,1)} %all-to-all-done.3) | data formatting | bytes 839680 | tf_op jit(solution)/shard_map/all_to_all | solution.py:153
  151.3 2.1 %convolution_bitcast_fusion.1 = f32[40,2,64,1,128]{4,2,1,0,3:T(8,128)S(1)} fusion(bf16[2,64,40,41]{1,0,3,2:T(2,128)(2,1)} %bitcast.127, bf16[40,41,64]{2,1,0:T(8,128)(2,1)} %get-tuple-element.26, bf16[40,41,64]{2,1,0:T(8,128)(2,1)S(1)} %get-tuple-element.25), kind=kOutput, calls=%fused_computation.14 | convolution fusion | flops 54579200 | bytes 3461120 | tf_op jit(solution)/shard_map/hfnrc,rcq->rhnfq/dot_general | solution.py:155
  153.5 1.8 %add_reduce_fusion = (f32[40,2,64]{2,1,0:T(2,128)S(1)}, f32[40,2,64]{2,1,0:T(2,128)S(1)}) fusion(f32[40,2,64,1,128]{4,2,1,0,3:T(8,128)S(1)} %convolution_bitcast_fusion.1, f32[40,64,64]{2,1,0:T(8,128)S(1)} %copy-done.1, f32[40,64,64]{2,1,0:T(8,128)S(1)} %get-tuple-element.27), kind=kLoop, calls=%fused_computation.1 | loop fusion | flops 2611200 | bytes 3973120 | tf_op jit(solution)/shard_map/reduce_sum | solution.py:93
  155.5 0.7 reshape.668
  156.2 10.3 %all-to-all-start.4 = ((bf16[16,2,320]{2,1,0:T(2,128)(2,1)}), bf16[16,2,320]{2,1,0:T(2,128)(2,1)S(1)}, u32[]{:S(2)}, u32[]{:S(2)}) async-start(bf16[16,2,320]{2,1,0:T(2,128)(2,1)} %reshape.668), calls=%async_computation.4 | async-start | bytes 49152 | tf_op jit(solution)/shard_map/all_to_all | solution.py:162
  166.6 1.8 %copy.95 = bf16[2,64,1,1640]{3,1,2,0:T(8,128)(2,1)} copy(bf16[2,64,1,1640]{3,0,1,2:T(2,128)(2,1)} %bitcast.29) | data formatting | bytes 839680
  168.5 5.5 %all-to-all-done.4 = bf16[16,2,320]{2,1,0:T(2,128)(2,1)S(1)} async-done(((bf16[16,2,320]{2,1,0:T(2,128)(2,1)}), bf16[16,2,320]{2,1,0:T(2,128)(2,1)S(1)}, u32[]{:S(2)}, u32[]{:S(2)}) %all-to-all-start.4) | async-done | bytes 20512 | tf_op jit(solution)/shard_map/all_to_all | solution.py:162
  174.3 0.5 fusion.38
  174.9 0.6 broadcast_select_fusion.2
  (76 shorter events, 2.9 us)
Async XLA Ops:
  0.6 2.2 %copy-start = (bf16[2,640,640]{2,1,0:T(8,128)(2,1)S(1)}, bf16[2,640,640]{2,1,0:T(8,128)(2,1)}, u32[]{:S(2)}) copy-start(bf16[2,640,640]{2,1,0:T(8,128)(2,1)} %param.12) | copy-start | bytes 4915204
  0.6 25.7 %copy-start.13 = (s32[32]{0:T(128)S(1)}, s32[32]{0:T(128)}, u32[]{:S(2)}) copy-start(s32[32]{0:T(128)} %param.10) | copy-start | bytes 388
  0.7 2.9 %copy-start.6 = (s32[640]{0:T(1024)S(1)}, s32[640]{0:T(1024)}, u32[]{:S(2)}) copy-start(s32[640]{0:T(1024)} %param.11) | copy-start | bytes 7684
  1.5 0.5 copy-start.9
  22.3 39.4 %all-to-all-start.1 = ((bf16[8,2,640]{2,1,0:T(2,128)(2,1)}), bf16[8,2,640]{2,1,0:T(2,128)(2,1)S(1)}, u32[]{:S(2)}, u32[]{:S(2)}) async-start(bf16[8,2,640]{2,1,0:T(2,128)(2,1)} %reshape.666), calls=%async_computation.1 | async-start | bytes 40960 | tf_op jit(solution)/shard_map/all_to_all | solution.py:27
  26.7 33.8 %copy-start.7 = (s32[64]{0:T(128)}, s32[64]{0:T(128)S(1)}, u32[]{:S(2)}) copy-start(s32[64]{0:T(128)S(1)} %mul.315) | copy-start | bytes 772
  64.2 2.3 %copy-start.2 = (bf16[40,41,64]{2,1,0:T(8,128)(2,1)S(1)}, bf16[40,41,64]{2,1,0:T(8,128)(2,1)}, u32[]{:S(2)}) copy-start(bf16[40,41,64]{2,1,0:T(8,128)(2,1)} %get-tuple-element.26) | copy-start | bytes 629764
  64.2 2.3 %copy-start.3 = (pred[40,64,41]{1,2,0:T(8,128)(4,1)S(1)}, pred[40,64,41]{1,2,0:T(8,128)(4,1)}, u32[]{:S(2)}) copy-start(pred[40,64,41]{1,2,0:T(8,128)(4,1)} %fusion.18) | copy-start | bytes 314884
  68.0 18.2 %copy-start.5 = (f32[2,1,1640]{2,1,0:T(1,128)S(1)}, f32[2,1,1640]{2,1,0:T(1,128)}, u32[]{:S(2)}) copy-start(f32[2,1,1640]{2,1,0:T(1,128)} %param.15) | copy-start | bytes 39364
  68.0 44.0 %copy-start.4 = (bf16[64,64]{1,0:T(8,128)(2,1)S(1)}, bf16[64,64]{1,0:T(8,128)(2,1)}, u32[]{:S(2)}) copy-start(bf16[64,64]{1,0:T(8,128)(2,1)} %param.14) | copy-start | bytes 24580
  73.0 49.7 %copy-start.8 = (s32[64]{0:T(128)S(1)}, s32[64]{0:T(128)}, u32[]{:S(2)}) copy-start(s32[64]{0:T(128)} %copy-done.7) | copy-start | bytes 772
  73.0 38.9 %all-to-all-start.2 = ((bf16[2,1,64,1640]{3,0,1,2:T(2,128)(2,1)}), bf16[2,1,64,1640]{3,0,1,2:T(2,128)(2,1)}, u32[]{:S(2)}, u32[]{:S(2)}) async-start(bf16[2,1,64,1640]{3,0,1,2:T(2,128)(2,1)} %copy.81), calls=%async_computation.2 | async-start | bytes 851968 | tf_op jit(solution)/shard_map/all_to_all | solution.py:147
  114.5 33.3 %all-to-all-start.3 = ((bf16[2,64,1,1640]{3,0,2,1:T(2,128)(2,1)}), bf16[2,64,1,1640]{3,0,2,1:T(2,128)(2,1)}, u32[]{:S(2)}, u32[]{:S(2)}) async-start(bf16[2,64,1,1640]{3,0,2,1:T(2,128)(2,1)} %copy.84), calls=%async_computation.3 | async-start | bytes 851968 | tf_op jit(solution)/shard_map/all_to_all | solution.py:153
  151.3 2.1 %copy-start.1 = (f32[40,64,64]{2,1,0:T(8,128)S(1)}, f32[40,64,64]{2,1,0:T(8,128)}, u32[]{:S(2)}) copy-start(f32[40,64,64]{2,1,0:T(8,128)} %get-tuple-element.28) | copy-start | bytes 1966084
  153.5 1.8 %copy-start.12 = (f32[40]{0:T(128)S(1)}, f32[40]{0:T(128)}, u32[]{:S(2)}) copy-start(f32[40]{0:T(128)} %get-tuple-element.15) | copy-start | bytes 484
  153.5 13.1 %copy-start.10 = (s32[2]{0:T(128)S(1)}, s32[2]{0:T(128)}, u32[]{:S(2)}) copy-start(s32[2]{0:T(128)} %copy-done.9) | copy-start | bytes 28
  155.2 19.0 %copy-start.11 = (f32[640]{0:T(1024)S(1)}, f32[640]{0:T(1024)}, u32[]{:S(2)}) copy-start(f32[640]{0:T(1024)} %param.13) | copy-start | bytes 7684
  156.2 17.7 %all-to-all-start.4 = ((bf16[16,2,320]{2,1,0:T(2,128)(2,1)}), bf16[16,2,320]{2,1,0:T(2,128)(2,1)S(1)}, u32[]{:S(2)}, u32[]{:S(2)}) async-start(bf16[16,2,320]{2,1,0:T(2,128)(2,1)} %reshape.668), calls=%async_computation.4 | async-start | bytes 49152 | tf_op jit(solution)/shard_map/all_to_all | solution.py:162
where the time goes:
time: 176 us
  waiting for transfers between devices  56.2 us (32%)
  other arithmetic  43.4 us (25%)
  starting transfers between devices  35 us (20%)
  blocking collectives  17.5 us (10%)
  local copies, waits for them, and re-layouts  16.6 us (9%)
  matrix products  5.77 us (3%)
    all_to_all x1, waiting for transfers between devices, per_device(): lax.all_to_all(local_grid, 'sect', split_axis=2, concat_axis=1, tiled=True)  25.7 us
    all_to_all x1, waiting for transfers between devices, per_device(): lax.all_to_all(tendency, 'sect', split_axis=1, concat_axis=2, tiled=True)  25 us
    cos x1, other arithmetic, sector_phases(): return (jnp.cos(outer_angle), jnp.sin(outer_angle), valid_mask)  19.3 us
    all_to_all x1, blocking collectives, exchange_in_order(): lax.all_to_all(parts, axes[k], split_axis=k, concat_axis=k, tiled=True)  17.5 us
    another operation x3, other arithmetic  16.9 us
    all_to_all x1, starting transfers between devices, per_device(): lax.all_to_all(local_grid, 'sect', split_axis=2, concat_axis=1, tiled=True)  13.2 us
    all_to_all x1, starting transfers between devices, per_device(): lax.all_to_all(analysis, WAVE, split_axis=3, concat_axis=4, tiled=True)  10.3 us
    all_to_all x1, starting transfers between devices, per_device(): lax.all_to_all(tendency, 'sect', split_axis=1, concat_axis=2, tiled=True)  8.18 us
  transfers between devices with their start and end apart: 4, of which 3 were waited for; matrix products, arithmetic and copies ran while one was open for 22% of the time, Pallas kernels for 0%

commit v1 on v0

v1 whole, which is shorter than its diff:
```python
import functools
import math

import jax
import jax.numpy as jnp
from jax import lax
from jax.experimental import pallas as pl
from jax.experimental.pallas import tpu as pltpu
from jax.sharding import Mesh
from jax.sharding import PartitionSpec as P

WAVE = ("wave_0", "wave_1")
NMAX = 640
ROWS = 40
SECW = 41
NSECT = 64
BANDS = 16
LANES = 128
GROUPS = 8
GROUP_ROWS = [[g, 15 - g, 16 + g, 31 - g, 32 + g] for g in range(GROUPS)]
SCALE = 2.0 / math.sqrt(40960.0)
F32 = jnp.float32
BF16 = jnp.bfloat16
SMEM = pltpu.SMEM


def lane_iota(shape):
    return lax.broadcasted_iota(jnp.int32, shape, len(shape) - 1)


def sincos_quarter(product, quarter):
    inverse = 1.0 / quarter
    turns = jnp.floor(product * inverse + 0.5)
    rest = product - turns * quarter
    theta = rest * (inverse * (0.5 * math.pi))
    sq = theta * theta
    sin_poly = theta + theta * sq * (
        -1.6666667163e-1 + sq * (8.3333337680e-3 + sq * (-1.9841270114e-4 + sq * 2.7557314297e-6))
    )
    cos_poly = 1.0 + sq * (
        -0.5 + sq * (4.1666667908e-2 + sq * (-1.3888889225e-3 + sq * (2.4801587642e-5 - sq * 2.7557314297e-7)))
    )
    return turns.astype(jnp.int32), cos_poly, sin_poly


def turn_cos(turn, cos_poly, sin_poly):
    value = jnp.where((turn & 1) == 1, sin_poly, cos_poly)
    return jnp.where(((turn + 1) & 2) == 2, -value, value)


def wave_lanes(low_ref, shape):
    lane = lane_iota(shape)
    low = jnp.zeros(shape, jnp.int32)
    for pair in range(32):
        low = jnp.where((lane >> 2) == pair, low_ref[pair], low)
    return jnp.where(((lane >> 1) & 1) == 0, low, NMAX - low)


def group_offsets(points_ref, first, group):
    found = []
    offset = jnp.int32(0)
    for row in GROUP_ROWS[group]:
        points = points_ref[first + row]
        width = (points + (NSECT - 1)) >> 6
        found.append((row, points, width, offset))
        offset = offset + width
    return found


def tables_kernel(rank_ref, low_ref, points_ref, factor_ref, u_ref, w_ref, trig_ref, slot_ref, pf_ref, scale_ref, pad_ref):
    first = rank_ref[0] * ROWS
    waves = wave_lanes(low_ref, (8, LANES))
    waves_f = waves.astype(F32)
    lane = lane_iota((NSECT, LANES))
    even = (lane & 1) == 0
    even_row = (lane_iota((1, LANES)) & 1) == 0
    sector = lax.broadcasted_iota(jnp.int32, (NSECT, LANES), 0).astype(F32)
    wave_row = waves_f[0:1]
    scale_ref[...] = jnp.zeros((LANES, LANES), F32)
    for half in range(ROWS // 2):
        row_a, row_b = 2 * half, 2 * half + 1
        points = jnp.where(even_row, points_ref[first + row_a], points_ref[first + row_b])
        width = (points + (NSECT - 1)) >> 6
        quarter = points.astype(F32) * 0.25
        step = wave_row * width.astype(F32)
        turn, cos_poly, sin_poly = sincos_quarter(sector * step, jnp.broadcast_to(quarter, (NSECT, LANES)))
        cos_ab = turn_cos(turn, cos_poly, sin_poly)
        sin_ab = turn_cos(turn + 3, cos_poly, sin_poly)
        cos_up = pltpu.roll(cos_ab, 1, axis=1)
        sin_up = pltpu.roll(sin_ab, 1, axis=1)
        cos_down = pltpu.roll(cos_ab, LANES - 1, axis=1)
        sin_down = pltpu.roll(sin_ab, LANES - 1, axis=1)
        u_ref[row_a] = jnp.where(even, cos_ab, sin_up)
        w_ref[row_a] = jnp.where(even, -sin_ab, cos_up)
        u_ref[row_b] = jnp.where(even, cos_down, sin_ab)
        w_ref[row_b] = jnp.where(even, -sin_down, cos_ab)
        for row in (row_a, row_b):
            length = jnp.full((1, LANES), points_ref[first + row], jnp.int32)
            keep = jnp.where(2 * waves[0:1] < length, (2.0 / SCALE) / length.astype(F32), 0.0)
            scale_ref[row : row + 1, :] = keep
            scale_ref[64 + row : 65 + row, :] = keep
    wave_col = jnp.transpose(jnp.broadcast_to(wave_row, (LANES, LANES)))
    part = lax.broadcasted_iota(jnp.int32, (LANES, LANES), 0) & 1
    slot = lane_iota((1, LANES))
    for h in range(2):
        pad_ref[h : h + 1, 0 : ROWS * SECW] = factor_ref[h]
    for group in range(GROUPS):
        which = jnp.full((1, LANES), -1, jnp.int32)
        column = jnp.zeros((1, LANES), jnp.int32)
        points = jnp.full((1, LANES), 20, jnp.int32)
        width = jnp.zeros((1, LANES), jnp.int32)
        packed = [jnp.zeros((1, LANES), F32), jnp.zeros((1, LANES), F32)]
        for i, (row, row_points, row_width, offset) in enumerate(group_offsets(points_ref, first, group)):
            mine = (slot >= offset) & (slot < offset + row_width)
            which = jnp.where(mine, i, which)
            column = jnp.where(mine, slot - offset, column)
            points = jnp.where(mine, row_points, points)
            width = jnp.where(mine, row_width, width)
            start = row * SECW
            base, shift = (start // LANES) * LANES, start % LANES
            for h in range(2):
                window = jnp.broadcast_to(pad_ref[h : h + 1, base : base + 2 * LANES], (8, 2 * LANES))
                window = pltpu.roll(window, 2 * LANES - shift, axis=1)[:, 0:LANES]
                window = pltpu.roll(window, offset & (LANES - 1), axis=1)
                packed[h] = jnp.where(mine, window[0:1], packed[h])
        slot_ref[0, group : group + 1, :] = which
        slot_ref[1, group : group + 1, :] = width
        slot_ref[2, group : group + 1, :] = points - column
        for h in range(2):
            pf_ref[h * GROUPS + group : h * GROUPS + group + 1, :] = packed[h]
        quarter = jnp.broadcast_to(points.astype(F32) * 0.25, (LANES, LANES))
        turn, cos_poly, sin_poly = sincos_quarter(wave_col * column.astype(F32), quarter)
        trig_ref[group] = turn_cos(turn + part, cos_poly, sin_poly).astype(BF16)


def synth_kernel(block_ref, u_ref, w_ref, trig_ref, slot_ref, out_ref, a_ref, b_ref, lhs_ref, row_ref):
    even = (lane_iota((LANES, LANES)) & 1) == 0
    coeffs = jnp.transpose(block_ref[...].astype(F32)) * SCALE
    a_ref[...] = jnp.where(even, coeffs, pltpu.roll(coeffs, 1, axis=1))
    b_ref[...] = jnp.where(even, pltpu.roll(coeffs, LANES - 1, axis=1), coeffs)
    sector = lax.broadcasted_iota(jnp.int32, (NSECT, LANES), 0)
    for group in range(GROUPS):
        for i, row in enumerate(GROUP_ROWS[group]):
            u = u_ref[row]
            w = w_ref[row]
            for h in range(2):
                at = h * 64 + row
                rot = a_ref[at : at + 1, :] * u + b_ref[at : at + 1, :] * w
                place = (i * 2 + h) * NSECT
                lhs_ref[place : place + NSECT, :] = rot.astype(BF16)
        product = jnp.dot(lhs_ref[...], trig_ref[group], preferred_element_type=F32)
        which = slot_ref[0, group : group + 1, :]
        valid = sector * slot_ref[1, group : group + 1, :] < slot_ref[2, group : group + 1, :]
        which = jnp.where(valid, which, -1)
        for h in range(2):
            total = jnp.zeros((NSECT, LANES), F32)
            for i in range(5):
                place = (i * 2 + h) * NSECT
                total = jnp.where(which == i, product[place : place + NSECT, :], total)
            row_ref[pl.ds(h * GROUPS + group, NSECT, stride=2 * GROUPS), :] = total
    out_ref[...] = row_ref[...].astype(BF16)


def tendency_kernel(grid_ref, couple_ref, pf_ref, out_ref, row_ref):
    row_ref[...] = grid_ref[...].astype(F32)
    couple = jnp.transpose(couple_ref[...].astype(F32)).astype(BF16)
    tends = []
    for line in range(2 * GROUPS):
        values = row_ref[pl.ds(line, NSECT, stride=2 * GROUPS), :].astype(BF16)
        coupled = jnp.dot(couple, values, preferred_element_type=F32)
        tends.append(coupled * pf_ref[line : line + 1, :])
    for line in range(2 * GROUPS):
        row_ref[pl.ds(line, NSECT, stride=2 * GROUPS), :] = tends[line]
    out_ref[...] = row_ref[...].astype(BF16)


def expand_kernel(rank_ref, points_ref, grid_ref, out_ref, row_ref, wide_ref):
    first = rank_ref[0] * ROWS
    row_ref[...] = grid_ref[...].astype(F32)
    lane = lane_iota((NSECT, LANES))
    tiles = -(-ROWS * SECW // LANES)
    info = {}
    for group in range(GROUPS):
        for row, _, width, offset in group_offsets(points_ref, first, group):
            info[row] = (group, width, offset)
    for h in range(2):
        for tile in range(tiles):
            total = jnp.zeros((NSECT, LANES), F32)
            for row in range(ROWS):
                start = row * SECW - tile * LANES
                if start >= LANES or start + SECW <= 0:
                    continue
                group, width, offset = info[row]
                values = row_ref[pl.ds(h * GROUPS + group, NSECT, stride=2 * GROUPS), :]
                values = pltpu.roll(values, (start + 2 * LANES - offset) & (LANES - 1), axis=1)
                total = jnp.where((lane >= start) & (lane < start + width), values, total)
            wide_ref[:, tile * LANES : (tile + 1) * LANES] = total
        out_ref[h] = wide_ref[:, 0 : ROWS * SECW].astype(BF16)


def analysis_kernel(tend_ref, u_ref, w_ref, trig_ref, slot_ref, scale_ref, out_ref, row_ref, lhs_ref, yu_ref, yw_ref):
    row_ref[...] = tend_ref[...].astype(F32)
    yu_ref[...] = jnp.zeros((LANES, LANES), F32)
    yw_ref[...] = jnp.zeros((LANES, LANES), F32)
    for group in range(GROUPS):
        which = slot_ref[0, group : group + 1, :]
        for h in range(2):
            values = row_ref[pl.ds(h * GROUPS + group, NSECT, stride=2 * GROUPS), :]
            for i in range(5):
                place = (i * 2 + h) * NSECT
                lhs_ref[place : place + NSECT, :] = jnp.where(which == i, values, 0.0).astype(BF16)
        product = lax.dot_general(
            lhs_ref[...], trig_ref[group], (((1,), (1,)), ((), ())), preferred_element_type=F32
        )
        for i, row in enumerate(GROUP_ROWS[group]):
            u = u_ref[row]
            w = w_ref[row]
            for h in range(2):
                place = (i * 2 + h) * NSECT
                sums = product[place : place + NSECT, :]
                at = h * 64 + row
                yu_ref[at : at + 1, :] = jnp.sum(sums * u, axis=0, keepdims=True)
                yw_ref[at : at + 1, :] = jnp.sum(sums * w, axis=0, keepdims=True)
    even = (lane_iota((LANES, LANES)) & 1) == 0
    yu = yu_ref[...]
    yw = yw_ref[...]
    real = yu + pltpu.roll(yu, LANES - 1, axis=1)
    imag = yw + pltpu.roll(yw, 1, axis=1)
    result = jnp.where(even, real, imag) * scale_ref[...]
    out_ref[...] = jnp.transpose(result).astype(BF16)


def slot_signs(low, shape):
    slot = lane_iota(shape)
    leading = slot < NMAX - low
    odd = jnp.where(leading, slot & 1, (slot + low) & 1) == 1
    return leading, odd


def legendre_kernel(rank_ref, low_ref, points_ref, spec_ref, leg_ref, out_ref, wide_ref):
    line = lax.broadcasted_iota(jnp.int32, (8, NMAX), 0)
    h = line >> 2
    member = (line >> 1) & 1
    part = line & 1
    points = points_ref[...]
    found = []
    for p in range(2):
        low = low_ref[2 * rank_ref[0] + p]
        leading, odd = slot_signs(low, (8, NMAX))
        spec = spec_ref[p].astype(F32)
        value = jnp.where(part == 0, spec[0:1], spec[1:2])
        value = jnp.where((member == 0) == leading, value, 0.0)
        value = jnp.where((h == 1) & odd, -value, value)
        product = jnp.dot(value.astype(BF16), leg_ref[p], preferred_element_type=F32)
        wave = jnp.where(member == 0, low, NMAX - low)
        found.append(jnp.where(2 * wave < points, product, 0.0))
    upper = line < 4
    wide_ref[...] = jnp.zeros((16, 6 * LANES), F32)
    wide_ref[0:8, 0:NMAX] = jnp.where(upper, found[0], pltpu.roll(found[1], 4, axis=0))
    wide_ref[8:16, 0:NMAX] = jnp.where(upper, pltpu.roll(found[0], 4, axis=0), found[1])
    lane = lane_iota((8, LANES))
    for band in range(BANDS):
        start = band * ROWS
        base, shift = (start // LANES) * LANES, start % LANES
        window = wide_ref[:, base : base + 2 * LANES]
        north = pltpu.roll(window[0:8], (2 * LANES - shift) % (2 * LANES), axis=1)[:, 0:LANES]
        south = pltpu.roll(window[8:16], (2 * LANES + 64 - shift) % (2 * LANES), axis=1)[:, 0:LANES]
        out_ref[band] = jnp.where(lane < 64, north, south).astype(BF16)


def project_kernel(rank_ref, low_ref, back_ref, gauss_ref, leg_ref, out_ref, wide_ref):
    lane = lane_iota((8, LANES))
    for tile in range(NMAX // LANES):
        north = jnp.zeros((8, LANES), F32)
        south = jnp.zeros((8, LANES), F32)
        for band in range(BANDS):
            start = band * ROWS - tile * LANES
            if start >= LANES or start + ROWS <= 0:
                continue
            block = back_ref[band].astype(F32)
            mine = (lane >= start) & (lane < start + ROWS)
            north = jnp.where(mine, pltpu.roll(block, start % LANES, axis=1), north)
            south = jnp.where(mine, pltpu.roll(block, (start + 64) % LANES, axis=1), south)
        wide_ref[0:8, tile * LANES : (tile + 1) * LANES] = north
        wide_ref[8:16, tile * LANES : (tile + 1) * LANES] = south
    north = wide_ref[0:8, :]
    south = wide_ref[8:16, :]
    gauss = gauss_ref[...]
    both = (north + south) * gauss
    less = (north - south) * gauss
    upper = lax.broadcasted_iota(jnp.int32, (8, NMAX), 0) < 4
    forms = [
        jnp.where(upper, both, pltpu.roll(less, 4, axis=0)),
        jnp.where(upper, pltpu.roll(both, 4, axis=0), less),
    ]
    for p in range(2):
        low = low_ref[2 * rank_ref[0] + p]
        leading, odd = slot_signs(low, (1, NMAX))
        product = lax.dot_general(
            forms[p].astype(BF16), leg_ref[p], (((1,), (1,)), ((), ())), preferred_element_type=F32
        )
        for r in range(2):
            lower = jnp.where(odd, product[4 + r : 5 + r], product[r : r + 1])
            higher = jnp.where(odd, product[6 + r : 7 + r], product[2 + r : 3 + r])
            out_ref[2 * p + r] = jnp.where(leading, lower, higher)


def whole():
    return pl.BlockSpec(memory_space=pltpu.VMEM)


def scalars():
    return pl.BlockSpec(memory_space=SMEM)


def run(kernel, name, outs, in_specs, scratch, *args):
    many = isinstance(outs, (list, tuple))
    return pl.pallas_call(
        kernel,
        out_shape=outs,
        in_specs=in_specs,
        out_specs=[whole() for _ in outs] if many else whole(),
        scratch_shapes=scratch,
        name=name,
    )(*args)


def struct(shape, dtype):
    return jax.ShapeDtypeStruct(shape, dtype)


def vmem(shape, dtype):
    return pltpu.VMEM(shape, dtype)


def make_tables(rank, pair_low, row_points, point_factor):
    return run(
        tables_kernel,
        "tables",
        [
            struct((ROWS, NSECT, LANES), F32),
            struct((ROWS, NSECT, LANES), F32),
            struct((GROUPS, LANES, LANES), BF16),
            struct((3, GROUPS, LANES), jnp.int32),
            struct((2 * GROUPS, LANES), F32),
            struct((LANES, LANES), F32),
        ],
        [scalars(), scalars(), scalars(), whole()],
        [vmem((8, 14 * LANES), F32)],
        rank, pair_low, row_points, point_factor,
    )


def synthesize(block, u, w, trig, slots):
    return run(
        synth_kernel,
        "synth",
        struct((NSECT * 2 * GROUPS, LANES), BF16),
        [whole()] * 5,
        [
            vmem((LANES, LANES), F32),
            vmem((LANES, LANES), F32),
            vmem((10 * NSECT, LANES), BF16),
            vmem((NSECT * 2 * GROUPS, LANES), F32),
        ],
        block.reshape(LANES, LANES), u, w, trig, slots,
    ).reshape(NSECT, 2 * GROUPS, LANES)


def tend_of(grid, couple, pf):
    return run(
        tendency_kernel,
        "tendency",
        struct((NSECT * 2 * GROUPS, LANES), BF16),
        [whole()] * 3,
        [vmem((NSECT * 2 * GROUPS, LANES), F32)],
        grid.reshape(-1, LANES), couple, pf,
    ).reshape(NSECT, 2 * GROUPS, LANES)


def expand(rank, row_points, grid):
    return run(
        expand_kernel,
        "expand",
        struct((2, NSECT, ROWS * SECW), BF16),
        [scalars(), scalars(), whole()],
        [vmem((NSECT * 2 * GROUPS, LANES), F32), vmem((NSECT, 13 * LANES), F32)],
        rank, row_points, grid.reshape(-1, LANES),
    )


def analyse(tend, u, w, trig, slots, scale):
    return run(
        analysis_kernel,
        "analysis",
        struct((LANES, LANES), BF16),
        [whole()] * 6,
        [
            vmem((NSECT * 2 * GROUPS, LANES), F32),
            vmem((10 * NSECT, LANES), BF16),
            vmem((LANES, LANES), F32),
            vmem((LANES, LANES), F32),
        ],
        tend.reshape(-1, LANES), u, w, trig, slots, scale,
    ).reshape(BANDS, 8, LANES)


def to_bands(rank, pair_low, row_points, spec, legendre):
    return run(
        legendre_kernel,
        "legendre",
        struct((BANDS, 8, LANES), BF16),
        [scalars(), scalars(), whole(), whole(), whole()],
        [vmem((16, 6 * LANES), F32)],
        rank, pair_low, row_points[None, :], spec, legendre,
    )


def project(rank, pair_low, back, gauss_weight, legendre):
    return run(
        project_kernel,
        "project",
        struct((4, 1, NMAX), F32),
        [scalars(), scalars(), whole(), whole(), whole()],
        [vmem((16, NMAX), F32)],
        rank, pair_low, back, gauss_weight[None, :], legendre,
    )


def cos_sin(product, points):
    quarter = points.astype(F32)[:, None, None] * 0.25
    turn, cos_poly, sin_poly = sincos_quarter(product.astype(F32), quarter)
    return turn_cos(turn, cos_poly, sin_poly), turn_cos(turn + 3, cos_poly, sin_poly)


def loose_path(block, rank, pair_low, row_points, couple, point_factor):
    fourier = block.reshape(BANDS, 2, 2, 2, 2, 64)[..., :ROWS]
    fourier = jnp.transpose(fourier, (0, 1, 2, 4, 3, 5)).reshape(64, 2, 2, ROWS).astype(F32)
    wave_list = jnp.stack([pair_low, NMAX - pair_low], axis=1).reshape(-1)
    points = lax.dynamic_slice_in_dim(row_points, rank[0] * ROWS, ROWS)
    width = (points + NSECT - 1) // NSECT
    columns = jnp.arange(SECW, dtype=jnp.int32)
    cos_inner, sin_inner = cos_sin(wave_list[None, None, :] * columns[None, :, None], points)
    trig = jnp.concatenate([cos_inner, -sin_inner], axis=2).astype(BF16)
    start = jnp.arange(NSECT, dtype=jnp.int32)[None, :] * width[:, None]
    cos_outer, sin_outer = cos_sin(wave_list[None, None, :] * start[:, :, None], points)
    valid = (columns < width[:, None, None]) & (start[:, :, None] + columns < points[:, None, None])
    real = jnp.transpose(fourier[:, :, 0], (2, 1, 0))[:, :, None]
    imag = jnp.transpose(fourier[:, :, 1], (2, 1, 0))[:, :, None]
    cos_wide, sin_wide = cos_outer[:, None], sin_outer[:, None]
    rotated = SCALE * jnp.concatenate(
        [real * cos_wide - imag * sin_wide, real * sin_wide + imag * cos_wide], axis=3
    )
    tile = jnp.einsum("rhnq,rcq->rhnc", rotated.astype(BF16), trig, preferred_element_type=F32)
    tile = jnp.where(valid[:, None], tile, 0.0).astype(BF16)
    local = jnp.transpose(tile, (2, 1, 0, 3)).reshape(NSECT, 2, ROWS * SECW)
    grid = lax.all_to_all(local, "sect", split_axis=0, concat_axis=0, tiled=True)
    coupled = jnp.einsum("fhx,fg->ghx", grid, couple, preferred_element_type=F32)
    tendency = (coupled * point_factor[None, :, 0]).astype(BF16)
    received = lax.all_to_all(tendency, "sect", split_axis=0, concat_axis=0, tiled=True)
    rows = received.reshape(NSECT, 2, ROWS, SECW)
    sums = jnp.einsum("nhrc,rcq->rhnq", rows, trig, preferred_element_type=F32)
    cos_part, sin_part = sums[..., :64], sums[..., 64:]
    real_sum = jnp.sum(cos_wide * cos_part + sin_wide * sin_part, axis=2)
    imag_sum = jnp.sum(cos_wide * sin_part - sin_wide * cos_part, axis=2)
    summed = jnp.stack([real_sum, imag_sum], axis=3)
    keep = 2 * wave_list[None, :] < points[:, None]
    scale = jnp.where(keep, 2.0 / (SCALE * points.astype(F32))[:, None], 0.0)
    analysis = (summed * scale[:, None, :, None]).astype(BF16)
    analysis = jnp.pad(analysis, ((0, 64 - ROWS), (0, 0), (0, 0), (0, 0)))
    analysis = jnp.transpose(analysis, (2, 3, 1, 0)).reshape(BANDS, 8, LANES)
    return jnp.transpose(grid, (1, 0, 2)), analysis


def rows_fit(row_points):
    width = ((row_points + NSECT - 1) // NSECT).reshape(BANDS, 5, GROUPS)
    total = width[:, 0] + width[:, 1, ::-1] + width[:, 2] + width[:, 3, ::-1] + width[:, 4]
    return jnp.max(total) <= LANES


def per_device(spec_in, pair_low, row_points, legendre, gauss_weight, couple, point_factor):
    rank = lax.axis_index(WAVE).astype(jnp.int32).reshape(1)
    outgoing = to_bands(rank, pair_low, row_points, spec_in[:, :, 0], legendre)
    block = lax.all_to_all(outgoing, WAVE, split_axis=0, concat_axis=0, tiled=True)
    u, w, trig, slots, pf, scale = make_tables(rank, pair_low, row_points, point_factor)

    def packed_path(block):
        local = synthesize(block, u, w, trig, slots)
        grid = lax.all_to_all(local, "sect", split_axis=0, concat_axis=0, tiled=True)
        tend = tend_of(grid, couple, pf)
        received = lax.all_to_all(tend, "sect", split_axis=0, concat_axis=0, tiled=True)
        return expand(rank, row_points, grid), analyse(received, u, w, trig, slots, scale)

    def every_slot(block):
        return loose_path(block, rank, pair_low, row_points, couple, point_factor)

    grid_field, analysis = lax.cond(rows_fit(row_points), packed_path, every_slot, block)
    back = lax.all_to_all(analysis, WAVE, split_axis=0, concat_axis=0, tiled=True)
    spec_out = project(rank, pair_low, back, gauss_weight, legendre)
    return grid_field[:, :, None, :], spec_out.reshape(2, 2, 1, NMAX)


def solution(mesh):
    split = Mesh(mesh.devices.reshape(8, 2, mesh.shape["sect"]), ("wave_0", "wave_1", "sect"))
    in_specs = (
        P(WAVE, None, "sect", None),
        P(),
        P(),
        P(WAVE, None, None),
        P(),
        P(),
        P(None, "sect", WAVE),
    )
    out_specs = (P(None, None, "sect", WAVE), P(WAVE, None, "sect", None))
    return jax.shard_map(
        per_device, mesh=split, in_specs=in_specs, out_specs=out_specs, check_vma=False
    )
```

time: 176 us -> 120 us (0.68)
  other arithmetic: 43.4 us -> 0.67 us
  waiting for transfers between devices: 56.2 us -> 22.4 us
  Pallas kernels: 0 us -> 22.3 us
  blocking collectives: 17.5 us -> 33.7 us
  local copies, waits for them, and re-layouts: 16.6 us -> 4.86 us
  matrix products: 5.77 us -> 0 us
    all_to_all x4 -> x3, waiting for transfers between devices: 56.2 us -> 22.4 us  [the longest x1 16.3 us: packed_path(): lax.all_to_all(tend, 'sect', split_axis=0, concat_axis=0, tiled=True)]
    pallas_call x0 -> x7, Pallas kernels: none -> 22.3 us  [run(): pl.pallas_call(kernel, out_shape=outs, in_specs=in_specs, out_specs=[whol...]
    cos x1 -> x0, other arithmetic: 19.3 us -> none  [sector_phases(): return (jnp.cos(outer_angle), jnp.sin(outer_angle), valid_mask)]
    another operation x6 -> x0, other arithmetic: 17.7 us -> none
    all_to_all x1, blocking collectives: 17.5 us -> 33.7 us  [packed_path(): lax.all_to_all(local, 'sect', split_axis=0, concat_axis=0, tiled=True)]
    dot_general x5 -> x0, matrix products: 5.77 us -> none  [the longest x1 2.14 us: per_device(): jnp.einsum('hfnrc,rcq->rhnfq', field_rows, trig_table, preferred_element_...]
    reshape x5 -> x1, local copies, waits for them, and re-layouts: 3.74 us -> 0.08 us  [rows_fit(): width = ((row_points + NSECT - 1) // NSECT).reshape(BANDS, 5, GROUPS)]
    unnamed x37 -> x8, local copies, waits for them, and re-layouts: 4.23 us -> 0.63 us
  transfers between devices with their start and end apart: 4 -> 3, of which waited for: 3 -> 2; matrix products, arithmetic and copies ran while one was open for 22% -> 2% of each run, Pallas kernels for 0% -> 7%
where the time goes in v1:
time: 120 us; the launch traced here: 119 us
  starting transfers between devices  33.9 us (28%)
  blocking collectives  33.7 us (28%)
  waiting for transfers between devices  22.4 us (19%)
  Pallas kernels  22.3 us (19%)
  local copies, waits for them, and re-layouts  4.86 us (4%)
  between operations  1.29 us (1%)
    all_to_all x1, blocking collectives, packed_path(): lax.all_to_all(local, 'sect', split_axis=0, concat_axis=0, tiled=True)  33.7 us
    pallas_call x7, Pallas kernels, run(): pl.pallas_call(kernel, out_shape=outs, in_specs=in_specs, out_specs=[whol...  22.3 us
    all_to_all x1, starting transfers between devices, per_device(): lax.all_to_all(outgoing, WAVE, split_axis=0, concat_axis=0, tiled=True)  17.4 us
    all_to_all x1, waiting for transfers between devices, packed_path(): lax.all_to_all(tend, 'sect', split_axis=0, concat_axis=0, tiled=True)  16.3 us
    all_to_all x1, starting transfers between devices, per_device(): lax.all_to_all(analysis, WAVE, split_axis=0, concat_axis=0, tiled=True)  9.93 us
    all_to_all x1, starting transfers between devices, packed_path(): lax.all_to_all(tend, 'sect', split_axis=0, concat_axis=0, tiled=True)  6.58 us
    all_to_all x1, waiting for transfers between devices, per_device(): lax.all_to_all(analysis, WAVE, split_axis=0, concat_axis=0, tiled=True)  6.11 us
  transfers between devices with their start and end apart: 3, of which 2 were waited for; matrix products, arithmetic and copies ran while one was open for 2% of the time, Pallas kernels for 7%

profile of v1, /device:TPU:1, one launch (start us, length us, event | category | flops | bytes accessed | tf_op | source)
XLA Modules:
  0.0 119.4 jit_solution(7701825343128630376)
XLA Ops:
  0.6 0.0 copy-start.8
  0.6 0.0 copy-start.15
  0.7 0.0 copy-start.12
  0.7 1.3 %broadcast_in_dim.30.points_ref = s32[1,640]{1,0:T(1,128)} reshape(s32[640]{0:T(1024)} %points_ref.1) | data formatting | bytes 5120 | tf_op jit(solution)/shard_map/broadcast_in_dim | solution.py:415
  2.0 2.5 %legendre.1 = bf16[16,8,128]{2,1,0:T(8,128)(2,1)} custom-call(s32[1]{0:T(128)} %bitcast.31.rank_ref, s32[32]{0:T(128)} %low_ref.5, s32[1,640]{1,0:T(1,128)} %broadcast_in_dim.30.points_ref, bf16[2,2,640]{2,1,0:T(2,128)(2,1)} %bitcast.72, bf16[2,640,640]{2,1,0:T(8,128)(2,1)} %leg_ref.3), custom_call_target="tpu_custom_call" | custom-call | tf_op jit(solution)/shard_map/legendre/pallas_call | solution.py:318
  4.5 17.4 %all-to-all-start.4 = ((bf16[16,8,128]{2,1,0:T(8,128)(2,1)}), bf16[16,8,128]{2,1,0:T(8,128)(2,1)S(1)}, u32[]{:S(2)}, u32[]{:S(2)}) async-start(bf16[16,8,128]{2,1,0:T(8,128)(2,1)} %legendre.1), calls=%async_computation.4 | async-start | bytes 65536 | tf_op jit(solution)/shard_map/all_to_all | solution.py:484
  21.9 0.0 copy-done.8
  21.9 0.0 copy-done.15
  21.9 0.0 copy-done.12
  21.9 6.1 %tables.1 = (f32[40,64,128]{2,1,0:T(8,128)}, f32[40,64,128]{2,1,0:T(8,128)}, bf16[8,128,128]{2,1,0:T(8,128)(2,1)}, s32[3,8,128]{2,1,0:T(8,128)}, f32[16,128]{1,0:T(8,128)}, /*index=5*/f32[128,128]{1,0:T(8,128)}) custom-call(s32[1]{0:T(128)} %bitcast.31.rank_ref, s32[32]{0:T(128)S(1)} %copy-done.15, s32[640]{0:T(1024)S(1)} %copy-done.8, ...), custom_call_target="tpu_custom_call" | custom-call | tf_op jit(solution)/shard_map/tables/pallas_call | solution.py:318
  28.0 0.1 reshape.238
  28.1 0.1 rev.6
  28.2 0.1 rev.7
  28.3 0.7 fusion.40
  29.6 0.0 all-to-all-done.4
  29.6 69.2 %conditional.1 = (bf16[16,8,128]{2,1,0:T(8,128)(2,1)}, bf16[2,64,1,1640]{3,1,2,0:T(8,128)(2,1)}) conditional(s32[]{:T(128)} %convert_element_type.67, (s32[32]{0:T(128)S(1)}, s32[]{:T(128)}, s32[640]{0:T(1024)S(1)}, bf16[16,8,128]{2,1,0:T(8,128)(2,1)S(1)}, bf16[64,64]{1,0:T(8,128)(2,1)}, /*index=5*/f32[2,1,1640]{2,1,0:T(1,128)}) %tuple.49, ...), branch_computations={%region_1.4_spmd, %region_4.5_spmd} | conditional | flops 156045088 | bytes 26824338 | solution.py:497
  29.8 0.6 copy-done.5
  30.4 3.7 %synth.1 = bf16[1024,128]{1,0:T(8,128)(2,1)} custom-call(bf16[128,128]{1,0:T(8,128)(2,1)} %bitcast.65, f32[40,64,128]{2,1,0:T(8,128)} %get-tuple-element.40.u_ref, f32[40,64,128]{2,1,0:T(8,128)} %get-tuple-element.41.w_ref, bf16[8,128,128]{2,1,0:T(8,128)(2,1)} %get-tuple-element.42.trig_ref, s32[3,8,128]{2,1,0:T(8,128)} %get-tuple-element.43.slot_ref), custom_call_target="tpu_custom_call" | custom-call | tf_op jit(solution)/shard_map/cond/branch_1_fun/synth/pallas_call | solution.py:318
  34.2 33.7 %all_to_all.26 = bf16[64,16,128]{2,1,0:T(8,128)(2,1)} all-to-all(bf16[64,16,128]{2,1,0:T(8,128)(2,1)} %bitcast.62), channel_id=1, replica_groups=mesh['wave_0'=8,'wave_1'=2,'sect'=64] {'sect'}, dimensions={0} | all-to-all | bytes 524288 | tf_op jit(solution)/shard_map/cond/branch_1_fun/all_to_all | solution.py:489
  67.8 2.1 %tendency.1 = bf16[1024,128]{1,0:T(8,128)(2,1)} custom-call(bf16[1024,128]{1,0:T(8,128)(2,1)} %bitcast.59, bf16[64,64]{1,0:T(8,128)(2,1)S(1)} %copy-done.11, f32[16,128]{1,0:T(8,128)S(1)} %copy-done.14), custom_call_target="tpu_custom_call" | custom-call | tf_op jit(solution)/shard_map/cond/branch_1_fun/tendency/pallas_call | solution.py:318
  69.9 6.6 %all-to-all-start.1 = ((bf16[64,16,128]{2,1,0:T(8,128)(2,1)}), bf16[64,16,128]{2,1,0:T(8,128)(2,1)S(1)}, u32[]{:S(2)}, u32[]{:S(2)}) async-start(bf16[64,16,128]{2,1,0:T(8,128)(2,1)} %bitcast.63), calls=%async_computation.1 | async-start | bytes 524288 | tf_op jit(solution)/shard_map/cond/branch_1_fun/all_to_all | solution.py:491
  76.5 2.5 %expand.1 = bf16[2,64,1640]{2,1,0:T(8,128)(2,1)} custom-call(s32[1]{0:T(128)} %get-tuple-element.47.rank_ref, s32[640]{0:T(1024)S(1)} %get-tuple-element.48.points_ref, bf16[1024,128]{1,0:T(8,128)(2,1)} %bitcast.60), custom_call_target="tpu_custom_call" | custom-call | tf_op jit(solution)/shard_map/cond/branch_1_fun/expand/pallas_call | solution.py:318
  79.0 16.3 %all-to-all-done.1 = bf16[64,16,128]{2,1,0:T(8,128)(2,1)S(1)} async-done(((bf16[64,16,128]{2,1,0:T(8,128)(2,1)}), bf16[64,16,128]{2,1,0:T(8,128)(2,1)S(1)}, u32[]{:S(2)}, u32[]{:S(2)}) %all-to-all-start.1) | async-done | bytes 262176 | tf_op jit(solution)/shard_map/cond/branch_1_fun/all_to_all | solution.py:491
  95.3 0.7 copy-done.4
  96.0 0.0 copy-done.1
  96.0 0.0 copy-done.3
  96.1 2.7 %analysis.1 = bf16[128,128]{1,0:T(8,128)(2,1)} custom-call(bf16[1024,128]{1,0:T(8,128)(2,1)} %bitcast.61, f32[40,64,128]{2,1,0:T(8,128)S(1)} %copy-done, f32[40,64,128]{2,1,0:T(8,128)S(1)} %copy-done.1, bf16[8,128,128]{2,1,0:T(8,128)(2,1)S(1)} %copy-done.3, s32[3,8,128]{2,1,0:T(8,128)S(1)} %copy-done.13, f32[128,128]{1,0:T(8,128)S(1)} %copy-done.9), custom_call_target="tpu_custom_call" | custom-call | tf_op jit(solution)/shard_map/cond/branch_1_fun/analysis/pallas_call | solution.py:318
  98.8 9.9 %all-to-all-start.5 = ((bf16[16,8,128]{2,1,0:T(8,128)(2,1)}), bf16[16,8,128]{2,1,0:T(8,128)(2,1)S(1)}, u32[]{:S(2)}, u32[]{:S(2)}) async-start(bf16[16,8,128]{2,1,0:T(8,128)(2,1)} %get-tuple-element.66), calls=%async_computation.5 | async-start | bytes 65536 | tf_op jit(solution)/shard_map/all_to_all | solution.py:498
  108.7 1.3 %broadcast_in_dim.35.gauss_ref = f32[1,640]{1,0:T(1,128)} reshape(f32[640]{0:T(1024)} %param.13) | data formatting | bytes 5120 | tf_op jit(solution)/shard_map/broadcast_in_dim | solution.py:426
  110.0 6.1 %all-to-all-done.5.back_ref = bf16[16,8,128]{2,1,0:T(8,128)(2,1)S(1)} async-done(((bf16[16,8,128]{2,1,0:T(8,128)(2,1)}), bf16[16,8,128]{2,1,0:T(8,128)(2,1)S(1)}, u32[]{:S(2)}, u32[]{:S(2)}) %all-to-all-start.5) | async-done | bytes 32800 | tf_op jit(solution)/shard_map/all_to_all | solution.py:498
  116.1 0.6 copy-done.6
  116.7 2.6 %project.1 = f32[4,1,640]{2,1,0:T(1,128)} custom-call(s32[1]{0:T(128)} %bitcast.31.rank_ref, s32[32]{0:T(128)} %low_ref.5, bf16[16,8,128]{2,1,0:T(8,128)(2,1)} %copy-done.6, f32[1,640]{1,0:T(1,128)} %broadcast_in_dim.35.gauss_ref, bf16[2,640,640]{2,1,0:T(8,128)(2,1)} %leg_ref.3), custom_call_target="tpu_custom_call" | custom-call | tf_op jit(solution)/shard_map/project/pallas_call | solution.py:318
  (17 shorter events, 0.1 us)
Async XLA Ops:
  0.6 21.3 %copy-start.8 = (s32[640]{0:T(1024)S(1)}, s32[640]{0:T(1024)}, u32[]{:S(2)}) copy-start(s32[640]{0:T(1024)} %points_ref.1) | copy-start | bytes 7684
  0.6 21.3 %copy-start.15 = (s32[32]{0:T(128)S(1)}, s32[32]{0:T(128)}, u32[]{:S(2)}) copy-start(s32[32]{0:T(128)} %low_ref.5) | copy-start | bytes 388
  0.7 21.3 %copy-start.12 = (f32[2,1,1640]{2,1,0:T(1,128)S(1)}, f32[2,1,1640]{2,1,0:T(1,128)}, u32[]{:S(2)}) copy-start(f32[2,1,1640]{2,1,0:T(1,128)} %factor_ref.1) | copy-start | bytes 39364
  4.5 25.1 %all-to-all-start.4 = ((bf16[16,8,128]{2,1,0:T(8,128)(2,1)}), bf16[16,8,128]{2,1,0:T(8,128)(2,1)S(1)}, u32[]{:S(2)}, u32[]{:S(2)}) async-start(bf16[16,8,128]{2,1,0:T(8,128)(2,1)} %legendre.1), calls=%async_computation.4 | async-start | bytes 65536 | tf_op jit(solution)/shard_map/all_to_all | solution.py:484
  29.8 0.6 copy-start.5
  30.4 37.4 %copy-start.11 = (bf16[64,64]{1,0:T(8,128)(2,1)S(1)}, bf16[64,64]{1,0:T(8,128)(2,1)}, u32[]{:S(2)}) copy-start(bf16[64,64]{1,0:T(8,128)(2,1)} %get-tuple-element.44.couple_ref) | copy-start | bytes 24580 | tf_op jit(solution)/shard_map/cond
  30.4 37.4 %copy-start.14 = (f32[16,128]{1,0:T(8,128)S(1)}, f32[16,128]{1,0:T(8,128)}, u32[]{:S(2)}) copy-start(f32[16,128]{1,0:T(8,128)} %get-tuple-element.45.pf_ref) | copy-start | bytes 24580 | tf_op jit(solution)/shard_map/cond
  30.4 65.6 %copy-start.1 = (f32[40,64,128]{2,1,0:T(8,128)S(1)}, f32[40,64,128]{2,1,0:T(8,128)}, u32[]{:S(2)}) copy-start(f32[40,64,128]{2,1,0:T(8,128)} %get-tuple-element.41.w_ref) | copy-start | bytes 3932164 | tf_op jit(solution)/shard_map/cond
  34.2 61.9 %copy-start = (f32[40,64,128]{2,1,0:T(8,128)S(1)}, f32[40,64,128]{2,1,0:T(8,128)}, u32[]{:S(2)}) copy-start(f32[40,64,128]{2,1,0:T(8,128)} %get-tuple-element.40.u_ref) | copy-start | bytes 3932164 | tf_op jit(solution)/shard_map/cond
  34.2 61.9 %copy-start.3 = (bf16[8,128,128]{2,1,0:T(8,128)(2,1)S(1)}, bf16[8,128,128]{2,1,0:T(8,128)(2,1)}, u32[]{:S(2)}) copy-start(bf16[8,128,128]{2,1,0:T(8,128)(2,1)} %get-tuple-element.42.trig_ref) | copy-start | bytes 786436 | tf_op jit(solution)/shard_map/cond
  34.2 61.9 %copy-start.9 = (f32[128,128]{1,0:T(8,128)S(1)}, f32[128,128]{1,0:T(8,128)}, u32[]{:S(2)}) copy-start(f32[128,128]{1,0:T(8,128)} %get-tuple-element.46.scale_ref) | copy-start | bytes 196612 | tf_op jit(solution)/shard_map/cond
  34.2 61.9 %copy-start.13 = (s32[3,8,128]{2,1,0:T(8,128)S(1)}, s32[3,8,128]{2,1,0:T(8,128)}, u32[]{:S(2)}) copy-start(s32[3,8,128]{2,1,0:T(8,128)} %get-tuple-element.43.slot_ref) | copy-start | bytes 36868 | tf_op jit(solution)/shard_map/cond
  69.9 25.4 %all-to-all-start.1 = ((bf16[64,16,128]{2,1,0:T(8,128)(2,1)}), bf16[64,16,128]{2,1,0:T(8,128)(2,1)S(1)}, u32[]{:S(2)}, u32[]{:S(2)}) async-start(bf16[64,16,128]{2,1,0:T(8,128)(2,1)} %bitcast.63), calls=%async_computation.1 | async-start | bytes 524288 | tf_op jit(solution)/shard_map/cond/branch_1_fun/all_to_all | solution.py:491
  95.3 0.7 copy-start.4
  98.8 17.3 %all-to-all-start.5 = ((bf16[16,8,128]{2,1,0:T(8,128)(2,1)}), bf16[16,8,128]{2,1,0:T(8,128)(2,1)S(1)}, u32[]{:S(2)}, u32[]{:S(2)}) async-start(bf16[16,8,128]{2,1,0:T(8,128)(2,1)} %get-tuple-element.66), calls=%async_computation.5 | async-start | bytes 65536 | tf_op jit(solution)/shard_map/all_to_all | solution.py:498
  116.1 0.6 copy-start.6

commit v2 on v1

--- a/solution.py
+++ b/solution.py
@@ -22,30 +22,36 @@
 F32 = jnp.float32
 BF16 = jnp.bfloat16
 SMEM = pltpu.SMEM
+GRANT = 12 * 2**20
 
 
 def lane_iota(shape):
     return lax.broadcasted_iota(jnp.int32, shape, len(shape) - 1)
 
 
-def sincos_quarter(product, quarter):
-    inverse = 1.0 / quarter
-    turns = jnp.floor(product * inverse + 0.5)
-    rest = product - turns * quarter
-    theta = rest * (inverse * (0.5 * math.pi))
-    sq = theta * theta
-    sin_poly = theta + theta * sq * (
-        -1.6666667163e-1 + sq * (8.3333337680e-3 + sq * (-1.9841270114e-4 + sq * 2.7557314297e-6))
-    )
-    cos_poly = 1.0 + sq * (
-        -0.5 + sq * (4.1666667908e-2 + sq * (-1.3888889225e-3 + sq * (2.4801587642e-5 - sq * 2.7557314297e-7)))
-    )
-    return turns.astype(jnp.int32), cos_poly, sin_poly
-
-
-def turn_cos(turn, cos_poly, sin_poly):
-    value = jnp.where((turn & 1) == 1, sin_poly, cos_poly)
-    return jnp.where(((turn + 1) & 2) == 2, -value, value)
+COS_TERMS = (6.52745434, -25.9667114, 60.1673855, -85.4501082, 64.9391157, -19.7392045, 0.999999989)
+SIN_TERMS = (3.23767246, -14.8995044, 42.0258325, -76.7030033, 81.6051307, -41.3417004, 6.2831853)
+
+
+def turn_part(product, points):
+    inverse = 1.0 / points
+    whole_turns = jnp.floor(product * inverse + 0.5)
+    return (product - whole_turns * points) * inverse
+
+
+def series(terms, square):
+    value = terms[0] * square + terms[1]
+    for term in terms[2:]:
+        value = value * square + term
+    return value
+
+
+def cos_turn(turn):
+    return series(COS_TERMS, turn * turn)
+
+
+def sin_turn(turn):
+    return turn * series(SIN_TERMS, turn * turn)
 
 
 def wave_lanes(low_ref, shape):
@@ -67,40 +73,32 @@
     return found
 
 
-def tables_kernel(rank_ref, low_ref, points_ref, factor_ref, u_ref, w_ref, trig_ref, slot_ref, pf_ref, scale_ref, pad_ref):
+def tables_kernel(rank_ref, low_ref, points_ref, factor_ref, coarse_ref, fine_ref, trig_ref, slot_ref, pf_ref, scale_ref, pad_ref):
     first = rank_ref[0] * ROWS
     waves = wave_lanes(low_ref, (8, LANES))
     waves_f = waves.astype(F32)
-    lane = lane_iota((NSECT, LANES))
-    even = (lane & 1) == 0
-    even_row = (lane_iota((1, LANES)) & 1) == 0
-    sector = lax.broadcasted_iota(jnp.int32, (NSECT, LANES), 0).astype(F32)
     wave_row = waves_f[0:1]
+    line = lax.broadcasted_iota(jnp.int32, (8, LANES), 0).astype(F32)
+    odd_lane = (lane_iota((8, LANES)) & 1).astype(F32)
+    fine_step = waves_f * line
+    coarse_step = fine_step * 8.0
+    back_quarter = odd_lane * 0.75
     scale_ref[...] = jnp.zeros((LANES, LANES), F32)
-    for half in range(ROWS // 2):
-        row_a, row_b = 2 * half, 2 * half + 1
-        points = jnp.where(even_row, points_ref[first + row_a], points_ref[first + row_b])
-        width = (points + (NSECT - 1)) >> 6
-        quarter = points.astype(F32) * 0.25
-        step = wave_row * width.astype(F32)
-        turn, cos_poly, sin_poly = sincos_quarter(sector * step, jnp.broadcast_to(quarter, (NSECT, LANES)))
-        cos_ab = turn_cos(turn, cos_poly, sin_poly)
-        sin_ab = turn_cos(turn + 3, cos_poly, sin_poly)
-        cos_up = pltpu.roll(cos_ab, 1, axis=1)
-        sin_up = pltpu.roll(sin_ab, 1, axis=1)
-        cos_down = pltpu.roll(cos_ab, LANES - 1, axis=1)
-        sin_down = pltpu.roll(sin_ab, LANES - 1, axis=1)
-        u_ref[row_a] = jnp.where(even, cos_ab, sin_up)
-        w_ref[row_a] = jnp.where(even, -sin_ab, cos_up)
-        u_ref[row_b] = jnp.where(even, cos_down, sin_ab)
-        w_ref[row_b] = jnp.where(even, -sin_down, cos_ab)
-        for row in (row_a, row_b):
-            length = jnp.full((1, LANES), points_ref[first + row], jnp.int32)
-            keep = jnp.where(2 * waves[0:1] < length, (2.0 / SCALE) / length.astype(F32), 0.0)
-            scale_ref[row : row + 1, :] = keep
-            scale_ref[64 + row : 65 + row, :] = keep
+    for row in range(ROWS):
+        length = jnp.full((8, LANES), points_ref[first + row], jnp.int32)
+        points = length.astype(F32)
+        width = ((length + (NSECT - 1)) >> 6).astype(F32)
+        fine = turn_part(fine_step * width, points)
+        fine_ref[0, row] = cos_turn(fine)
+        fine_ref[1, row] = sin_turn(fine)
+        coarse = turn_part(coarse_step * width + back_quarter * points, points)
+        coarse_ref[0, row] = cos_turn(coarse)
+        coarse_ref[1, row] = -sin_turn(coarse)
+        keep = jnp.where(2 * waves < length, (2.0 / SCALE) / points, 0.0)[0:1]
+        scale_ref[row : row + 1, :] = keep
+        scale_ref[64 + row : 65 + row, :] = keep
     wave_col = jnp.transpose(jnp.broadcast_to(wave_row, (LANES, LANES)))
-    part = lax.broadcasted_iota(jnp.int32, (LANES, LANES), 0) & 1
+    quarter = (lax.broadcasted_iota(jnp.int32, (LANES, LANES), 0) & 1).astype(F32) * 0.25
     slot = lane_iota((1, LANES))
     for h in range(2):
         pad_ref[h : h + 1, 0 : ROWS * SECW] = factor_ref[h]
@@ -109,7 +107,7 @@
         column = jnp.zeros((1, LANES), jnp.int32)
         points = jnp.full((1, LANES), 20, jnp.int32)
         width = jnp.zeros((1, LANES), jnp.int32)
-        packed = [jnp.zeros((1, LANES), F32), jnp.zeros((1, LANES), F32)]
+        packed = jnp.zeros((8, LANES), F32)
         for i, (row, row_points, row_width, offset) in enumerate(group_offsets(points_ref, first, group)):
             mine = (slot >= offset) & (slot < offset + row_width)
             which = jnp.where(mine, i, which)
@@ -118,36 +116,42 @@
             width = jnp.where(mine, row_width, width)
             start = row * SECW
             base, shift = (start // LANES) * LANES, start % LANES
-            for h in range(2):
-                window = jnp.broadcast_to(pad_ref[h : h + 1, base : base + 2 * LANES], (8, 2 * LANES))
-                window = pltpu.roll(window, 2 * LANES - shift, axis=1)[:, 0:LANES]
-                window = pltpu.roll(window, offset & (LANES - 1), axis=1)
-                packed[h] = jnp.where(mine, window[0:1], packed[h])
+            window = pltpu.roll(pad_ref[:, base : base + 2 * LANES], 2 * LANES - shift, axis=1)[:, 0:LANES]
+            packed = jnp.where(mine, pltpu.roll(window, offset & (LANES - 1), axis=1), packed)
         slot_ref[0, group : group + 1, :] = which
         slot_ref[1, group : group + 1, :] = width
         slot_ref[2, group : group + 1, :] = points - column
         for h in range(2):
-            pf_ref[h * GROUPS + group : h * GROUPS + group + 1, :] = packed[h]
-        quarter = jnp.broadcast_to(points.astype(F32) * 0.25, (LANES, LANES))
-        turn, cos_poly, sin_poly = sincos_quarter(wave_col * column.astype(F32), quarter)
-        trig_ref[group] = turn_cos(turn + part, cos_poly, sin_poly).astype(BF16)
-
-
-def synth_kernel(block_ref, u_ref, w_ref, trig_ref, slot_ref, out_ref, a_ref, b_ref, lhs_ref, row_ref):
+            pf_ref[h, group : group + 1, :] = packed[h : h + 1]
+        points = jnp.broadcast_to(points.astype(F32), (LANES, LANES))
+        turn = turn_part(wave_col * column.astype(F32) + quarter * points, points)
+        trig_ref[group] = cos_turn(turn).astype(BF16)
+
+
+def synth_kernel(block_ref, coarse_ref, fine_ref, trig_ref, slot_ref, scale_ref, out_ref, a_ref, b_ref, lhs_ref, row_ref):
     even = (lane_iota((LANES, LANES)) & 1) == 0
-    coeffs = jnp.transpose(block_ref[...].astype(F32)) * SCALE
+    coeffs = jnp.transpose(block_ref[...].reshape(LANES, LANES).astype(F32))
+    coeffs = jnp.where(scale_ref[...] > 0.0, coeffs, 0.0) * SCALE
     a_ref[...] = jnp.where(even, coeffs, pltpu.roll(coeffs, 1, axis=1))
     b_ref[...] = jnp.where(even, pltpu.roll(coeffs, LANES - 1, axis=1), coeffs)
     sector = lax.broadcasted_iota(jnp.int32, (NSECT, LANES), 0)
     for group in range(GROUPS):
         for i, row in enumerate(GROUP_ROWS[group]):
-            u = u_ref[row]
-            w = w_ref[row]
+            cos = fine_ref[0, row]
+            sin = fine_ref[1, row]
             for h in range(2):
                 at = h * 64 + row
-                rot = a_ref[at : at + 1, :] * u + b_ref[at : at + 1, :] * w
-                place = (i * 2 + h) * NSECT
-                lhs_ref[place : place + NSECT, :] = rot.astype(BF16)
+                a = a_ref[at : at + 1, :]
+                b = b_ref[at : at + 1, :]
+                near = a * cos - b * sin
+                far = a * sin + b * cos
+                for block in range(0, 8, 2):
+                    pair = [
+                        coarse_ref[0, row, k : k + 1, :] * near + coarse_ref[1, row, k : k + 1, :] * far
+                        for k in (block, block + 1)
+                    ]
+                    place = (i * 2 + h) * NSECT + block * 8
+                    lhs_ref[place : place + 16, :] = jnp.concatenate(pair, axis=0).astype(BF16)
         product = jnp.dot(lhs_ref[...], trig_ref[group], preferred_element_type=F32)
         which = slot_ref[0, group : group + 1, :]
         valid = sector * slot_ref[1, group : group + 1, :] < slot_ref[2, group : group + 1, :]
@@ -158,25 +162,30 @@
                 place = (i * 2 + h) * NSECT
                 total = jnp.where(which == i, product[place : place + NSECT, :], total)
             row_ref[pl.ds(h * GROUPS + group, NSECT, stride=2 * GROUPS), :] = total
-    out_ref[...] = row_ref[...].astype(BF16)
+    out_ref[...] = row_ref[...].astype(BF16).reshape(NSECT, 2 * GROUPS, LANES)
+
+
+def rows_of(ref):
+    return ref[...].reshape(NSECT * 2 * GROUPS, LANES).astype(F32)
 
 
 def tendency_kernel(grid_ref, couple_ref, pf_ref, out_ref, row_ref):
-    row_ref[...] = grid_ref[...].astype(F32)
+    row_ref[...] = rows_of(grid_ref)
     couple = jnp.transpose(couple_ref[...].astype(F32)).astype(BF16)
     tends = []
     for line in range(2 * GROUPS):
         values = row_ref[pl.ds(line, NSECT, stride=2 * GROUPS), :].astype(BF16)
         coupled = jnp.dot(couple, values, preferred_element_type=F32)
-        tends.append(coupled * pf_ref[line : line + 1, :])
+        h, group = divmod(line, GROUPS)
+        tends.append(coupled * pf_ref[h, group : group + 1, :])
     for line in range(2 * GROUPS):
         row_ref[pl.ds(line, NSECT, stride=2 * GROUPS), :] = tends[line]
-    out_ref[...] = row_ref[...].astype(BF16)
+    out_ref[...] = row_ref[...].astype(BF16).reshape(NSECT, 2 * GROUPS, LANES)
 
 
 def expand_kernel(rank_ref, points_ref, grid_ref, out_ref, row_ref, wide_ref):
     first = rank_ref[0] * ROWS
-    row_ref[...] = grid_ref[...].astype(F32)
+    row_ref[...] = rows_of(grid_ref)
     lane = lane_iota((NSECT, LANES))
     tiles = -(-ROWS * SECW // LANES)
     info = {}
@@ -198,8 +207,8 @@
         out_ref[h] = wide_ref[:, 0 : ROWS * SECW].astype(BF16)
 
 
-def analysis_kernel(tend_ref, u_ref, w_ref, trig_ref, slot_ref, scale_ref, out_ref, row_ref, lhs_ref, yu_ref, yw_ref):
-    row_ref[...] = tend_ref[...].astype(F32)
+def analysis_kernel(tend_ref, coarse_ref, fine_ref, trig_ref, slot_ref, scale_ref, out_ref, row_ref, lhs_ref, yu_ref, yw_ref):
+    row_ref[...] = rows_of(tend_ref)
     yu_ref[...] = jnp.zeros((LANES, LANES), F32)
     yw_ref[...] = jnp.zeros((LANES, LANES), F32)
     for group in range(GROUPS):
@@ -213,21 +222,26 @@
             lhs_ref[...], trig_ref[group], (((1,), (1,)), ((), ())), preferred_element_type=F32
         )
         for i, row in enumerate(GROUP_ROWS[group]):
-            u = u_ref[row]
-            w = w_ref[row]
+            cos = fine_ref[0, row]
+            sin = fine_ref[1, row]
             for h in range(2):
-                place = (i * 2 + h) * NSECT
-                sums = product[place : place + NSECT, :]
+                near = jnp.zeros((8, LANES), F32)
+                far = jnp.zeros((8, LANES), F32)
+                for block in range(8):
+                    place = (i * 2 + h) * NSECT + block * 8
+                    sums = product[place : place + 8, :]
+                    near = near + sums * coarse_ref[0, row, block : block + 1, :]
+                    far = far + sums * coarse_ref[1, row, block : block + 1, :]
                 at = h * 64 + row
-                yu_ref[at : at + 1, :] = jnp.sum(sums * u, axis=0, keepdims=True)
-                yw_ref[at : at + 1, :] = jnp.sum(sums * w, axis=0, keepdims=True)
+                yu_ref[at : at + 1, :] = jnp.sum(near * cos + far * sin, axis=0, keepdims=True)
+                yw_ref[at : at + 1, :] = jnp.sum(far * cos - near * sin, axis=0, keepdims=True)
     even = (lane_iota((LANES, LANES)) & 1) == 0
     yu = yu_ref[...]
     yw = yw_ref[...]
     real = yu + pltpu.roll(yu, LANES - 1, axis=1)
     imag = yw + pltpu.roll(yw, 1, axis=1)
     result = jnp.where(even, real, imag) * scale_ref[...]
-    out_ref[...] = jnp.transpose(result).astype(BF16)
+    out_ref[...] = jnp.transpose(result).astype(BF16).reshape(BANDS, 8, LANES)
 
 
 def slot_signs(low, shape):
@@ -237,12 +251,11 @@
     return leading, odd
 
 
-def legendre_kernel(rank_ref, low_ref, points_ref, spec_ref, leg_ref, out_ref, wide_ref):
+def legendre_kernel(rank_ref, low_ref, spec_ref, leg_ref, out_ref, wide_ref):
     line = lax.broadcasted_iota(jnp.int32, (8, NMAX), 0)
     h = line >> 2
     member = (line >> 1) & 1
     part = line & 1
-    points = points_ref[...]
     found = []
     for p in range(2):
         low = low_ref[2 * rank_ref[0] + p]
@@ -251,9 +264,7 @@
         value = jnp.where(part == 0, spec[0:1], spec[1:2])
         value = jnp.where((member == 0) == leading, value, 0.0)
         value = jnp.where((h == 1) & odd, -value, value)
-        product = jnp.dot(value.astype(BF16), leg_ref[p], preferred_element_type=F32)
-        wave = jnp.where(member == 0, low, NMAX - low)
-        found.append(jnp.where(2 * wave < points, product, 0.0))
+        found.append(jnp.dot(value.astype(BF16), leg_ref[p], preferred_element_type=F32))
     upper = line < 4
     wide_ref[...] = jnp.zeros((16, 6 * LANES), F32)
     wide_ref[0:8, 0:NMAX] = jnp.where(upper, found[0], pltpu.roll(found[1], 4, axis=0))
@@ -321,6 +332,7 @@
         in_specs=in_specs,
         out_specs=[whole() for _ in outs] if many else whole(),
         scratch_shapes=scratch,
+        compiler_params=pltpu.CompilerParams(vmem_limit_bytes=GRANT),
         name=name,
     )(*args)
 
@@ -338,11 +350,11 @@
         tables_kernel,
         "tables",
         [
-            struct((ROWS, NSECT, LANES), F32),
-            struct((ROWS, NSECT, LANES), F32),
+            struct((2, ROWS, 8, LANES), F32),
+            struct((2, ROWS, 8, LANES), F32),
             struct((GROUPS, LANES, LANES), BF16),
             struct((3, GROUPS, LANES), jnp.int32),
-            struct((2 * GROUPS, LANES), F32),
+            struct((2, GROUPS, LANES), F32),
             struct((LANES, LANES), F32),
         ],
         [scalars(), scalars(), scalars(), whole()],
@@ -351,31 +363,35 @@
     )
 
 
-def synthesize(block, u, w, trig, slots):
+PACKED = (NSECT, 2 * GROUPS, LANES)
+LINES = NSECT * 2 * GROUPS
+
+
+def synthesize(block, coarse, fine, trig, slots, scale):
     return run(
         synth_kernel,
         "synth",
-        struct((NSECT * 2 * GROUPS, LANES), BF16),
-        [whole()] * 5,
+        struct(PACKED, BF16),
+        [whole()] * 6,
         [
             vmem((LANES, LANES), F32),
             vmem((LANES, LANES), F32),
             vmem((10 * NSECT, LANES), BF16),
-            vmem((NSECT * 2 * GROUPS, LANES), F32),
+            vmem((LINES, LANES), F32),
         ],
-        block.reshape(LANES, LANES), u, w, trig, slots,
-    ).reshape(NSECT, 2 * GROUPS, LANES)
+        block, coarse, fine, trig, slots, scale,
+    )
 
 
 def tend_of(grid, couple, pf):
     return run(
         tendency_kernel,
         "tendency",
-        struct((NSECT * 2 * GROUPS, LANES), BF16),
+        struct(PACKED, BF16),
         [whole()] * 3,
-        [vmem((NSECT * 2 * GROUPS, LANES), F32)],
-        grid.reshape(-1, LANES), couple, pf,
-    ).reshape(NSECT, 2 * GROUPS, LANES)
+        [vmem((LINES, LANES), F32)],
+        grid, couple, pf,
+    )
 
 
 def expand(rank, row_points, grid):
@@ -384,35 +400,35 @@
         "expand",
         struct((2, NSECT, ROWS * SECW), BF16),
         [scalars(), scalars(), whole()],
-        [vmem((NSECT * 2 * GROUPS, LANES), F32), vmem((NSECT, 13 * LANES), F32)],
-        rank, row_points, grid.reshape(-1, LANES),
-    )
-
-
-def analyse(tend, u, w, trig, slots, scale):
+        [vmem((LINES, LANES), F32), vmem((NSECT, 13 * LANES), F32)],
+        rank, row_points, grid,
+    )
+
+
+def analyse(tend, coarse, fine, trig, slots, scale):
     return run(
         analysis_kernel,
         "analysis",
-        struct((LANES, LANES), BF16),
+        struct((BANDS, 8, LANES), BF16),
         [whole()] * 6,
         [
-            vmem((NSECT * 2 * GROUPS, LANES), F32),
+            vmem((LINES, LANES), F32),
             vmem((10 * NSECT, LANES), BF16),
             vmem((LANES, LANES), F32),
             vmem((LANES, LANES), F32),
         ],
-        tend.reshape(-1, LANES), u, w, trig, slots, scale,
-    ).reshape(BANDS, 8, LANES)
-
-
-def to_bands(rank, pair_low, row_points, spec, legendre):
+        tend, coarse, fine, trig, slots, scale,
+    )
+
+
+def to_bands(rank, pair_low, spec, legendre):
     return run(
         legendre_kernel,
         "legendre",
         struct((BANDS, 8, LANES), BF16),
-        [scalars(), scalars(), whole(), whole(), whole()],
+        [scalars(), scalars(), whole(), whole()],
         [vmem((16, 6 * LANES), F32)],
-        rank, pair_low, row_points[None, :], spec, legendre,
+        rank, pair_low, spec, legendre,
     )
 
 
@@ -428,9 +444,8 @@
 
 
 def cos_sin(product, points):
-    quarter = points.astype(F32)[:, None, None] * 0.25
-    turn, cos_poly, sin_poly = sincos_quarter(product.astype(F32), quarter)
-    return turn_cos(turn, cos_poly, sin_poly), turn_cos(turn + 3, cos_poly, sin_poly)
+    turn = turn_part(product.astype(F32), points.astype(F32)[:, None, None])
+    return cos_turn(turn), sin_turn(turn)
 
 
 def loose_path(block, rank, pair_low, row_points, couple, point_factor):
@@ -445,6 +460,8 @@
     start = jnp.arange(NSECT, dtype=jnp.int32)[None, :] * width[:, None]
     cos_outer, sin_outer = cos_sin(wave_list[None, None, :] * start[:, :, None], points)
     valid = (columns < width[:, None, None]) & (start[:, :, None] + columns < points[:, None, None])
+    keep = 2 * wave_list[None, :] < points[:, None]
+    fourier = jnp.where(jnp.transpose(keep)[:, None, None], fourier, 0.0)
     real = jnp.transpose(fourier[:, :, 0], (2, 1, 0))[:, :, None]
     imag = jnp.transpose(fourier[:, :, 1], (2, 1, 0))[:, :, None]
     cos_wide, sin_wide = cos_outer[:, None], sin_outer[:, None]
@@ -464,7 +481,6 @@
     real_sum = jnp.sum(cos_wide * cos_part + sin_wide * sin_part, axis=2)
     imag_sum = jnp.sum(cos_wide * sin_part - sin_wide * cos_part, axis=2)
     summed = jnp.stack([real_sum, imag_sum], axis=3)
-    keep = 2 * wave_list[None, :] < points[:, None]
     scale = jnp.where(keep, 2.0 / (SCALE * points.astype(F32))[:, None], 0.0)
     analysis = (summed * scale[:, None, :, None]).astype(BF16)
     analysis = jnp.pad(analysis, ((0, 64 - ROWS), (0, 0), (0, 0), (0, 0)))
@@ -480,16 +496,17 @@
 
 def per_device(spec_in, pair_low, row_points, legendre, gauss_weight, couple, point_factor):
     rank = lax.axis_index(WAVE).astype(jnp.int32).reshape(1)
-    outgoing = to_bands(rank, pair_low, row_points, spec_in[:, :, 0], legendre)
+    outgoing = to_bands(rank, pair_low, spec_in[:, :, 0], legendre)
     block = lax.all_to_all(outgoing, WAVE, split_axis=0, concat_axis=0, tiled=True)
-    u, w, trig, slots, pf, scale = make_tables(rank, pair_low, row_points, point_factor)
+    coarse, fine, trig, slots, pf, scale = make_tables(rank, pair_low, row_points, point_factor)
+
+    def cross(x):
+        return lax.all_to_all(x, "sect", split_axis=0, concat_axis=0, tiled=True)
 
     def packed_path(block):
-        local = synthesize(block, u, w, trig, slots)
-        grid = lax.all_to_all(local, "sect", split_axis=0, concat_axis=0, tiled=True)
-        tend = tend_of(grid, couple, pf)
-        received = lax.all_to_all(tend, "sect", split_axis=0, concat_axis=0, tiled=True)
-        return expand(rank, row_points, grid), analyse(received, u, w, trig, slots, scale)
+        grid = cross(synthesize(block, coarse, fine, trig, slots, scale))
+        received = cross(tend_of(grid, couple, pf))
+        return expand(rank, row_points, grid), analyse(received, coarse, fine, trig, slots, scale)
 
     def every_slot(block):
         return loose_path(block, rank, pair_low, row_points, couple, point_factor)

time: 120 us -> 110 us (0.917)
  Pallas kernels: 22.3 us -> 13.3 us
  waiting for transfers between devices: 22.4 us -> 27.5 us
  starting transfers between devices: 33.9 us -> 31.2 us
  local copies, waits for them, and re-layouts: 4.86 us -> 2.48 us
    pallas_call x7, Pallas kernels: 22.3 us -> 13.3 us  [run(): pl.pallas_call(kernel, out_shape=outs, in_specs=in_specs, out_specs=[whol...]
    all_to_all x1, waiting for transfers between devices: 0.01 us -> 3.54 us  [per_device(): lax.all_to_all(outgoing, WAVE, split_axis=0, concat_axis=0, tiled=True)]
    all_to_all x1, starting transfers between devices: 9.93 us -> 6.88 us  [per_device(): lax.all_to_all(analysis, WAVE, split_axis=0, concat_axis=0, tiled=True)]
    unnamed x8 -> x16, local copies, waits for them, and re-layouts: 0.63 us -> 2.15 us
    cond x18 -> x6, local copies, waits for them, and re-layouts: 1.33 us -> 0.01 us
    broadcast_in_dim x1 -> x0, local copies, waits for them, and re-layouts: 1.3 us -> none  [to_bands(): row_points[None, :]]
    broadcast_in_dim x1, local copies, waits for them, and re-layouts: 1.28 us -> 0.01 us  [project(): gauss_weight[None, :]]
    all_to_all x1, waiting for transfers between devices: 6.11 us -> 7.37 us  [per_device(): lax.all_to_all(analysis, WAVE, split_axis=0, concat_axis=0, tiled=True)]
  transfers between devices with their start and end apart: 3 -> 3, of which waited for: 2 -> 3; matrix products, arithmetic and copies ran while one was open for 2% -> 1% of each run, Pallas kernels for 7% -> 4%
where the time goes in v2:
time: 110 us
  blocking collectives  32.8 us (30%)
  starting transfers between devices  31.2 us (28%)
  waiting for transfers between devices  27.5 us (25%)
  Pallas kernels  13.3 us (12%)
  local copies, waits for them, and re-layouts  2.48 us (2%)
  between operations  1.39 us (1%)
    all_to_all x1, blocking collectives, cross(): return lax.all_to_all(x, 'sect', split_axis=0, concat_axis=0, tiled=True)  32.8 us
    all_to_all x1, starting transfers between devices, per_device(): lax.all_to_all(outgoing, WAVE, split_axis=0, concat_axis=0, tiled=True)  17.4 us
    all_to_all x1, waiting for transfers between devices, cross(): return lax.all_to_all(x, 'sect', split_axis=0, concat_axis=0, tiled=True)  16.6 us
    pallas_call x7, Pallas kernels, run(): pl.pallas_call(kernel, out_shape=outs, in_specs=in_specs, out_specs=[whol...  13.3 us
    all_to_all x1, waiting for transfers between devices, per_device(): lax.all_to_all(analysis, WAVE, split_axis=0, concat_axis=0, tiled=True)  7.37 us
    all_to_all x1, starting transfers between devices, cross(): return lax.all_to_all(x, 'sect', split_axis=0, concat_axis=0, tiled=True)  6.95 us
    all_to_all x1, starting transfers between devices, per_device(): lax.all_to_all(analysis, WAVE, split_axis=0, concat_axis=0, tiled=True)  6.88 us
    all_to_all x1, waiting for transfers between devices, per_device(): lax.all_to_all(outgoing, WAVE, split_axis=0, concat_axis=0, tiled=True)  3.54 us
  transfers between devices with their start and end apart: 3, of which 3 were waited for; matrix products, arithmetic and copies ran while one was open for 1% of the time, Pallas kernels for 4%

profile of v2, /device:TPU:1, one launch (start us, length us, event | category | flops | bytes accessed | tf_op | source)
XLA Modules:
  0.0 109.5 jit_solution(4961400326732211093)
XLA Ops:
  0.6 0.0 copy-start.11
  0.6 0.0 copy-start.10
  0.7 0.0 copy-start.8
  0.7 0.0 copy-start
  0.7 1.4 %copy-done = bf16[2,640,640]{2,1,0:T(8,128)(2,1)S(1)} copy-done((bf16[2,640,640]{2,1,0:T(8,128)(2,1)S(1)}, bf16[2,640,640]{2,1,0:T(8,128)(2,1)}, u32[]{:S(2)}) %copy-start) | copy-done | bytes 1638424
  2.1 0.7 copy-done.2
  2.8 1.8 %legendre.1 = bf16[16,8,128]{2,1,0:T(8,128)(2,1)} custom-call(s32[1]{0:T(128)} %bitcast.23.rank_ref, s32[32]{0:T(128)} %low_ref.5, bf16[2,2,640]{2,1,0:T(2,128)(2,1)S(1)} %bitcast.47, bf16[2,640,640]{2,1,0:T(8,128)(2,1)S(1)} %copy-done), custom_call_target="tpu_custom_call" | custom-call | tf_op jit(solution)/shard_map/legendre/pallas_call | solution.py:329
  4.6 17.4 %all-to-all-start.4 = ((bf16[16,8,128]{2,1,0:T(8,128)(2,1)}), bf16[16,8,128]{2,1,0:T(8,128)(2,1)S(1)}, u32[]{:S(2)}, u32[]{:S(2)}) async-start(bf16[16,8,128]{2,1,0:T(8,128)(2,1)} %legendre.1), calls=%async_computation.4 | async-start | bytes 65536 | tf_op jit(solution)/shard_map/all_to_all | solution.py:500
  22.0 0.0 copy-done.10
  22.1 0.0 copy-done.11
  22.1 0.0 copy-done.9
  22.1 2.2 %tables.1 = (f32[2,40,8,128]{3,2,1,0:T(8,128)}, f32[2,40,8,128]{3,2,1,0:T(8,128)}, bf16[8,128,128]{2,1,0:T(8,128)(2,1)}, s32[3,8,128]{2,1,0:T(8,128)S(1)}, f32[2...) custom-call(s32[1]{0:T(128)} %bitcast.23.rank_ref, s32[32]{0:T(128)S(1)} %copy-done.11, s32[640]{0:T(1024)S(1)} %copy-done.10, ...), custom_call_target="tpu_custom_call" | custom-call | tf_op jit(solution)/shard_map/tables/pallas_call | solution.py:329
  24.3 0.1 reshape.226
  24.4 0.1 rev.6
  24.5 0.1 rev.7
  24.6 0.7 fusion.34
  26.0 3.5 %all-to-all-done.4 = bf16[16,8,128]{2,1,0:T(8,128)(2,1)S(1)} async-done(((bf16[16,8,128]{2,1,0:T(8,128)(2,1)}), bf16[16,8,128]{2,1,0:T(8,128)(2,1)S(1)}, u32[]{:S(2)}, u32[]{:S(2)}) %all-to-all-start.4) | async-done | bytes 32800 | tf_op jit(solution)/shard_map/all_to_all | solution.py:500
  29.5 0.0 copy-done.8
  29.5 64.0 %conditional.1 = (bf16[16,8,128]{2,1,0:T(8,128)(2,1)}, bf16[2,64,1,1640]{3,1,2,0:T(8,128)(2,1)}) conditional(s32[]{:T(128)} %convert_element_type.54, (s32[32]{0:T(128)S(1)}, s32[]{:T(128)}, s32[640]{0:T(1024)S(1)}, bf16[16,8,128]{2,1,0:T(8,128)(2,1)S(1)}, bf16[64,64]{1,0:T(8,128)(2,1)S(1)}, /*index=5*/f32[2,1,1640]{2,1,0:T(1,128)S(1)}) %tuple.51, ...), branch_computations={%region_1.4_spmd, %region_4.5_spmd} | conditional | flops 151992576 | bytes 32076330 | solution.py:514
  29.5 2.4 %synth.1 = bf16[64,16,128]{2,1,0:T(8,128)(2,1)S(1)} custom-call(bf16[16,8,128]{2,1,0:T(8,128)(2,1)S(1)} %get-tuple-element.39.block_ref, f32[2,40,8,128]{3,2,1,0:T(8,128)} %get-tuple-element.40.coarse_ref, f32[2,40,8,128]{3,2,1,0:T(8,128)} %get-tuple-element.41.fine_ref, bf16[8,128,128]{2,1,0:T(8,128)(2,1)} %get-tuple-element.42.trig_ref, ...), custom_call_target="tpu_custom_call" | custom-call | tf_op jit(solution)/shard_map/cond/branch_1_fun/synth/pallas_call | solution.py:329
  32.0 32.8 %all_to_all.26.grid_ref = bf16[64,16,128]{2,1,0:T(8,128)(2,1)S(1)} all-to-all(bf16[64,16,128]{2,1,0:T(8,128)(2,1)S(1)} %synth.1), channel_id=1, replica_groups=mesh['wave_0'=8,'wave_1'=2,'sect'=64] {'sect'}, dimensions={0} | all-to-all | bytes 524288 | tf_op jit(solution)/shard_map/cond/branch_1_fun/all_to_all | solution.py:504
  64.8 1.1 %tendency.1 = bf16[64,16,128]{2,1,0:T(8,128)(2,1)} custom-call(bf16[64,16,128]{2,1,0:T(8,128)(2,1)S(1)} %all_to_all.26.grid_ref, bf16[64,64]{1,0:T(8,128)(2,1)S(1)} %get-tuple-element.45.couple_ref, f32[2,8,128]{2,1,0:T(8,128)S(1)} %get-tuple-element.46.pf_ref), custom_call_target="tpu_custom_call" | custom-call | tf_op jit(solution)/shard_map/cond/branch_1_fun/tendency/pallas_call | solution.py:329
  66.0 6.9 %all-to-all-start.1 = ((bf16[64,16,128]{2,1,0:T(8,128)(2,1)}), bf16[64,16,128]{2,1,0:T(8,128)(2,1)S(1)}, u32[]{:S(2)}, u32[]{:S(2)}) async-start(bf16[64,16,128]{2,1,0:T(8,128)(2,1)} %tendency.1), calls=%async_computation.1 | async-start | bytes 524288 | tf_op jit(solution)/shard_map/cond/branch_1_fun/all_to_all | solution.py:504
  72.9 2.1 %expand.1 = bf16[2,64,1640]{2,1,0:T(8,128)(2,1)} custom-call(s32[1]{0:T(128)} %get-tuple-element.47.rank_ref, s32[640]{0:T(1024)S(1)} %get-tuple-element.48.points_ref, bf16[64,16,128]{2,1,0:T(8,128)(2,1)S(1)} %all_to_all.26.grid_ref), custom_call_target="tpu_custom_call" | custom-call | tf_op jit(solution)/shard_map/cond/branch_1_fun/expand/pallas_call | solution.py:329
  75.0 16.6 %all-to-all-done.1.tend_ref = bf16[64,16,128]{2,1,0:T(8,128)(2,1)S(1)} async-done(((bf16[64,16,128]{2,1,0:T(8,128)(2,1)}), bf16[64,16,128]{2,1,0:T(8,128)(2,1)S(1)}, u32[]{:S(2)}, u32[]{:S(2)}) %all-to-all-start.1) | async-done | bytes 262176 | tf_op jit(solution)/shard_map/cond/branch_1_fun/all_to_all | solution.py:504
  91.7 0.0 copy-done.5
  91.7 1.8 %analysis.1 = bf16[16,8,128]{2,1,0:T(8,128)(2,1)} custom-call(bf16[64,16,128]{2,1,0:T(8,128)(2,1)S(1)} %all-to-all-done.1.tend_ref, f32[2,40,8,128]{3,2,1,0:T(8,128)S(1)} %copy-done.5, f32[2,40,8,128]{3,2,1,0:T(8,128)S(1)} %copy-done.6, bf16[8,128,128]{2,1,0:T(8,128)(2,1)S(1)} %copy-done.7, s32[3,8,128]{2,1,0:T(8,128)S(1)} %get-tuple-element.43.slot_ref, ...), custom_call_target="tpu_custom_call" | custom-call | tf_op jit(solution)/shard_map/cond/branch_1_fun/analysis/pallas_call | solution.py:329
  93.5 6.9 %all-to-all-start.5 = ((bf16[16,8,128]{2,1,0:T(8,128)(2,1)}), bf16[16,8,128]{2,1,0:T(8,128)(2,1)S(1)}, u32[]{:S(2)}, u32[]{:S(2)}) async-start(bf16[16,8,128]{2,1,0:T(8,128)(2,1)} %get-tuple-element.66), calls=%async_computation.5 | async-start | bytes 65536 | tf_op jit(solution)/shard_map/all_to_all | solution.py:515
  100.4 0.0 copy-done.12
  100.4 7.4 %all-to-all-done.5.back_ref = bf16[16,8,128]{2,1,0:T(8,128)(2,1)S(1)} async-done(((bf16[16,8,128]{2,1,0:T(8,128)(2,1)}), bf16[16,8,128]{2,1,0:T(8,128)(2,1)S(1)}, u32[]{:S(2)}, u32[]{:S(2)}) %all-to-all-start.5) | async-done | bytes 32800 | tf_op jit(solution)/shard_map/all_to_all | solution.py:515
  107.8 0.0 copy-done.1
  107.8 1.7 %project.1 = f32[4,1,640]{2,1,0:T(1,128)} custom-call(s32[1]{0:T(128)} %bitcast.23.rank_ref, s32[32]{0:T(128)S(1)} %copy-done.11, bf16[16,8,128]{2,1,0:T(8,128)(2,1)S(1)} %all-to-all-done.5.back_ref, f32[1,640]{1,0:T(1,128)S(1)} %broadcast_in_dim.64.gauss_ref, bf16[2,640,640]{2,1,0:T(8,128)(2,1)S(1)} %copy-done.1), custom_call_target="tpu_custom_call" | custom-call | tf_op jit(solution)/shard_map/project/pallas_call | solution.py:329
  (12 shorter events, 0.0 us)
Async XLA Ops:
  0.6 21.4 %copy-start.11 = (s32[32]{0:T(128)S(1)}, s32[32]{0:T(128)}, u32[]{:S(2)}) copy-start(s32[32]{0:T(128)} %low_ref.5) | copy-start | bytes 388
  0.6 21.4 %copy-start.10 = (s32[640]{0:T(1024)S(1)}, s32[640]{0:T(1024)}, u32[]{:S(2)}) copy-start(s32[640]{0:T(1024)} %points_ref.1) | copy-start | bytes 7684
  0.7 28.9 %copy-start.8 = (bf16[64,64]{1,0:T(8,128)(2,1)S(1)}, bf16[64,64]{1,0:T(8,128)(2,1)}, u32[]{:S(2)}) copy-start(bf16[64,64]{1,0:T(8,128)(2,1)} %param.14) | copy-start | bytes 24580
  0.7 1.4 %copy-start = (bf16[2,640,640]{2,1,0:T(8,128)(2,1)S(1)}, bf16[2,640,640]{2,1,0:T(8,128)(2,1)}, u32[]{:S(2)}) copy-start(bf16[2,640,640]{2,1,0:T(8,128)(2,1)} %leg_ref.3) | copy-start | bytes 4915204
  2.1 0.7 copy-start.2
  2.8 19.3 %copy-start.9 = (f32[2,1,1640]{2,1,0:T(1,128)S(1)}, f32[2,1,1640]{2,1,0:T(1,128)}, u32[]{:S(2)}) copy-start(f32[2,1,1640]{2,1,0:T(1,128)} %factor_ref.1) | copy-start | bytes 39364
  4.6 24.9 %all-to-all-start.4 = ((bf16[16,8,128]{2,1,0:T(8,128)(2,1)}), bf16[16,8,128]{2,1,0:T(8,128)(2,1)S(1)}, u32[]{:S(2)}, u32[]{:S(2)}) async-start(bf16[16,8,128]{2,1,0:T(8,128)(2,1)} %legendre.1), calls=%async_computation.4 | async-start | bytes 65536 | tf_op jit(solution)/shard_map/all_to_all | solution.py:500
  29.5 70.9 %copy-start.12 = (f32[640]{0:T(1024)S(1)}, f32[640]{0:T(1024)}, u32[]{:S(2)}) copy-start(f32[640]{0:T(1024)} %param.13) | copy-start | bytes 7684
  29.5 78.3 %copy-start.1 = (bf16[2,640,640]{2,1,0:T(8,128)(2,1)S(1)}, bf16[2,640,640]{2,1,0:T(8,128)(2,1)}, u32[]{:S(2)}) copy-start(bf16[2,640,640]{2,1,0:T(8,128)(2,1)} %leg_ref.3) | copy-start | bytes 4915204
  32.0 59.7 %copy-start.5 = (f32[2,40,8,128]{3,2,1,0:T(8,128)S(1)}, f32[2,40,8,128]{3,2,1,0:T(8,128)}, u32[]{:S(2)}) copy-start(f32[2,40,8,128]{3,2,1,0:T(8,128)} %get-tuple-element.40.coarse_ref) | copy-start | bytes 983044 | tf_op jit(solution)/shard_map/cond
  32.0 59.7 %copy-start.6 = (f32[2,40,8,128]{3,2,1,0:T(8,128)S(1)}, f32[2,40,8,128]{3,2,1,0:T(8,128)}, u32[]{:S(2)}) copy-start(f32[2,40,8,128]{3,2,1,0:T(8,128)} %get-tuple-element.41.fine_ref) | copy-start | bytes 983044 | tf_op jit(solution)/shard_map/cond
  32.0 59.7 %copy-start.7 = (bf16[8,128,128]{2,1,0:T(8,128)(2,1)S(1)}, bf16[8,128,128]{2,1,0:T(8,128)(2,1)}, u32[]{:S(2)}) copy-start(bf16[8,128,128]{2,1,0:T(8,128)(2,1)} %get-tuple-element.42.trig_ref) | copy-start | bytes 786436 | tf_op jit(solution)/shard_map/cond
  66.0 25.7 %all-to-all-start.1 = ((bf16[64,16,128]{2,1,0:T(8,128)(2,1)}), bf16[64,16,128]{2,1,0:T(8,128)(2,1)S(1)}, u32[]{:S(2)}, u32[]{:S(2)}) async-start(bf16[64,16,128]{2,1,0:T(8,128)(2,1)} %tendency.1), calls=%async_computation.1 | async-start | bytes 524288 | tf_op jit(solution)/shard_map/cond/branch_1_fun/all_to_all | solution.py:504
  93.5 14.3 %all-to-all-start.5 = ((bf16[16,8,128]{2,1,0:T(8,128)(2,1)}), bf16[16,8,128]{2,1,0:T(8,128)(2,1)S(1)}, u32[]{:S(2)}, u32[]{:S(2)}) async-start(bf16[16,8,128]{2,1,0:T(8,128)(2,1)} %get-tuple-element.66), calls=%async_computation.5 | async-start | bytes 65536 | tf_op jit(solution)/shard_map/all_to_all | solution.py:515

commit v3 on v2

--- a/solution.py
+++ b/solution.py
@@ -16,13 +16,27 @@
 NSECT = 64
 BANDS = 16
 LANES = 128
-GROUPS = 8
-GROUP_ROWS = [[g, 15 - g, 16 + g, 31 - g, 32 + g] for g in range(GROUPS)]
+GROUP_ROWS = [
+    [0, 7, 16, 22, 31, 34],
+    [9, 12, 25, 26, 39],
+    [2, 10, 15, 20, 29, 36],
+    [11, 18, 19, 32, 33],
+    [4, 6, 13, 24, 28, 37],
+    [1, 8, 14, 23, 30, 35],
+    [3, 5, 17, 21, 27, 38],
+]
+GROUPS = len(GROUP_ROWS)
+MOST = max(len(rows) for rows in GROUP_ROWS)
 SCALE = 2.0 / math.sqrt(40960.0)
 F32 = jnp.float32
 BF16 = jnp.bfloat16
 SMEM = pltpu.SMEM
 GRANT = 12 * 2**20
+FULL_GRANT = 60 * 1024 * 2**10
+
+
+def wave_rank():
+    return lax.axis_index(WAVE).astype(jnp.int32)
 
 
 def lane_iota(shape):
@@ -73,8 +87,8 @@
     return found
 
 
-def tables_kernel(rank_ref, low_ref, points_ref, factor_ref, coarse_ref, fine_ref, trig_ref, slot_ref, pf_ref, scale_ref, pad_ref):
-    first = rank_ref[0] * ROWS
+def tables_kernel(low_ref, points_ref, factor_ref, coarse_ref, fine_ref, trig_ref, slot_ref, pf_ref, scale_ref, pad_ref):
+    first = wave_rank() * ROWS
     waves = wave_lanes(low_ref, (8, LANES))
     waves_f = waves.astype(F32)
     wave_row = waves_f[0:1]
@@ -136,6 +150,7 @@
     b_ref[...] = jnp.where(even, pltpu.roll(coeffs, LANES - 1, axis=1), coeffs)
     sector = lax.broadcasted_iota(jnp.int32, (NSECT, LANES), 0)
     for group in range(GROUPS):
+        used = 2 * NSECT * len(GROUP_ROWS[group])
         for i, row in enumerate(GROUP_ROWS[group]):
             cos = fine_ref[0, row]
             sin = fine_ref[1, row]
@@ -152,21 +167,21 @@
                     ]
                     place = (i * 2 + h) * NSECT + block * 8
                     lhs_ref[place : place + 16, :] = jnp.concatenate(pair, axis=0).astype(BF16)
-        product = jnp.dot(lhs_ref[...], trig_ref[group], preferred_element_type=F32)
+        product = jnp.dot(lhs_ref[0:used, :], trig_ref[group], preferred_element_type=F32)
         which = slot_ref[0, group : group + 1, :]
         valid = sector * slot_ref[1, group : group + 1, :] < slot_ref[2, group : group + 1, :]
         which = jnp.where(valid, which, -1)
         for h in range(2):
             total = jnp.zeros((NSECT, LANES), F32)
-            for i in range(5):
+            for i in range(len(GROUP_ROWS[group])):
                 place = (i * 2 + h) * NSECT
                 total = jnp.where(which == i, product[place : place + NSECT, :], total)
-            row_ref[pl.ds(h * GROUPS + group, NSECT, stride=2 * GROUPS), :] = total
-    out_ref[...] = row_ref[...].astype(BF16).reshape(NSECT, 2 * GROUPS, LANES)
+            row_ref[pl.ds(2 * group + h, NSECT, stride=2 * GROUPS), :] = total
+    out_ref[...] = row_ref[...].astype(BF16)
 
 
 def rows_of(ref):
-    return ref[...].reshape(NSECT * 2 * GROUPS, LANES).astype(F32)
+    return ref[...].astype(F32)
 
 
 def tendency_kernel(grid_ref, couple_ref, pf_ref, out_ref, row_ref):
@@ -176,15 +191,15 @@
     for line in range(2 * GROUPS):
         values = row_ref[pl.ds(line, NSECT, stride=2 * GROUPS), :].astype(BF16)
         coupled = jnp.dot(couple, values, preferred_element_type=F32)
-        h, group = divmod(line, GROUPS)
+        group, h = divmod(line, 2)
         tends.append(coupled * pf_ref[h, group : group + 1, :])
     for line in range(2 * GROUPS):
         row_ref[pl.ds(line, NSECT, stride=2 * GROUPS), :] = tends[line]
-    out_ref[...] = row_ref[...].astype(BF16).reshape(NSECT, 2 * GROUPS, LANES)
-
-
-def expand_kernel(rank_ref, points_ref, grid_ref, out_ref, row_ref, wide_ref):
-    first = rank_ref[0] * ROWS
+    out_ref[...] = row_ref[...].astype(BF16)
+
+
+def expand_kernel(points_ref, grid_ref, out_ref, row_ref, wide_ref):
+    first = wave_rank() * ROWS
     row_ref[...] = rows_of(grid_ref)
     lane = lane_iota((NSECT, LANES))
     tiles = -(-ROWS * SECW // LANES)
@@ -200,7 +215,7 @@
                 if start >= LANES or start + SECW <= 0:
                     continue
                 group, width, offset = info[row]
-                values = row_ref[pl.ds(h * GROUPS + group, NSECT, stride=2 * GROUPS), :]
+                values = row_ref[pl.ds(2 * group + h, NSECT, stride=2 * GROUPS), :]
                 values = pltpu.roll(values, (start + 2 * LANES - offset) & (LANES - 1), axis=1)
                 total = jnp.where((lane >= start) & (lane < start + width), values, total)
             wide_ref[:, tile * LANES : (tile + 1) * LANES] = total
@@ -213,13 +228,14 @@
     yw_ref[...] = jnp.zeros((LANES, LANES), F32)
     for group in range(GROUPS):
         which = slot_ref[0, group : group + 1, :]
+        used = 2 * NSECT * len(GROUP_ROWS[group])
         for h in range(2):
-            values = row_ref[pl.ds(h * GROUPS + group, NSECT, stride=2 * GROUPS), :]
-            for i in range(5):
+            values = row_ref[pl.ds(2 * group + h, NSECT, stride=2 * GROUPS), :]
+            for i in range(len(GROUP_ROWS[group])):
                 place = (i * 2 + h) * NSECT
                 lhs_ref[place : place + NSECT, :] = jnp.where(which == i, values, 0.0).astype(BF16)
         product = lax.dot_general(
-            lhs_ref[...], trig_ref[group], (((1,), (1,)), ((), ())), preferred_element_type=F32
+            lhs_ref[0:used, :], trig_ref[group], (((1,), (1,)), ((), ())), preferred_element_type=F32
         )
         for i, row in enumerate(GROUP_ROWS[group]):
             cos = fine_ref[0, row]
@@ -251,22 +267,36 @@
     return leading, odd
 
 
-def legendre_kernel(rank_ref, low_ref, spec_ref, leg_ref, out_ref, wide_ref):
+def legendre_kernel(low_ref, spec_hbm, leg_hbm, out_ref, wide_ref, spec_ref, leg_ref, sems):
+    half = NMAX // 2
+    spec_copy = pltpu.make_async_copy(spec_hbm, spec_ref, sems.at[4])
+    spec_copy.start()
+    leg_copies = []
+    for p in range(2):
+        for part in range(2):
+            rows = pl.ds(part * half, half)
+            leg_copies.append(
+                pltpu.make_async_copy(leg_hbm.at[p, rows], leg_ref.at[p, rows], sems.at[2 * p + part])
+            )
+            leg_copies[-1].start()
+    wide_ref[...] = jnp.zeros((16, 6 * LANES), F32)
+    spec_copy.wait()
     line = lax.broadcasted_iota(jnp.int32, (8, NMAX), 0)
     h = line >> 2
     member = (line >> 1) & 1
     part = line & 1
     found = []
     for p in range(2):
-        low = low_ref[2 * rank_ref[0] + p]
+        low = low_ref[2 * wave_rank() + p]
         leading, odd = slot_signs(low, (8, NMAX))
         spec = spec_ref[p].astype(F32)
         value = jnp.where(part == 0, spec[0:1], spec[1:2])
         value = jnp.where((member == 0) == leading, value, 0.0)
         value = jnp.where((h == 1) & odd, -value, value)
+        leg_copies[2 * p].wait()
+        leg_copies[2 * p + 1].wait()
         found.append(jnp.dot(value.astype(BF16), leg_ref[p], preferred_element_type=F32))
     upper = line < 4
-    wide_ref[...] = jnp.zeros((16, 6 * LANES), F32)
     wide_ref[0:8, 0:NMAX] = jnp.where(upper, found[0], pltpu.roll(found[1], 4, axis=0))
     wide_ref[8:16, 0:NMAX] = jnp.where(upper, pltpu.roll(found[0], 4, axis=0), found[1])
     lane = lane_iota((8, LANES))
@@ -279,7 +309,7 @@
         out_ref[band] = jnp.where(lane < 64, north, south).astype(BF16)
 
 
-def project_kernel(rank_ref, low_ref, back_ref, gauss_ref, leg_ref, out_ref, wide_ref):
+def project_kernel(low_ref, back_ref, gauss_ref, leg_ref, out_ref, wide_ref):
     lane = lane_iota((8, LANES))
     for tile in range(NMAX // LANES):
         north = jnp.zeros((8, LANES), F32)
@@ -305,7 +335,7 @@
         jnp.where(upper, pltpu.roll(both, 4, axis=0), less),
     ]
     for p in range(2):
-        low = low_ref[2 * rank_ref[0] + p]
+        low = low_ref[2 * wave_rank() + p]
         leading, odd = slot_signs(low, (1, NMAX))
         product = lax.dot_general(
             forms[p].astype(BF16), leg_ref[p], (((1,), (1,)), ((), ())), preferred_element_type=F32
@@ -320,11 +350,15 @@
     return pl.BlockSpec(memory_space=pltpu.VMEM)
 
 
+def in_hbm():
+    return pl.BlockSpec(memory_space=pltpu.HBM)
+
+
 def scalars():
     return pl.BlockSpec(memory_space=SMEM)
 
 
-def run(kernel, name, outs, in_specs, scratch, *args):
+def run(kernel, name, outs, in_specs, scratch, *args, grant=GRANT):
     many = isinstance(outs, (list, tuple))
     return pl.pallas_call(
         kernel,
@@ -332,7 +366,7 @@
         in_specs=in_specs,
         out_specs=[whole() for _ in outs] if many else whole(),
         scratch_shapes=scratch,
-        compiler_params=pltpu.CompilerParams(vmem_limit_bytes=GRANT),
+        compiler_params=pltpu.CompilerParams(vmem_limit_bytes=grant),
         name=name,
     )(*args)
 
@@ -345,7 +379,7 @@
     return pltpu.VMEM(shape, dtype)
 
 
-def make_tables(rank, pair_low, row_points, point_factor):
+def make_tables(pair_low, row_points, point_factor):
     return run(
         tables_kernel,
         "tables",
@@ -357,13 +391,12 @@
             struct((2, GROUPS, LANES), F32),
             struct((LANES, LANES), F32),
         ],
-        [scalars(), scalars(), scalars(), whole()],
+        [scalars(), scalars(), whole()],
         [vmem((8, 14 * LANES), F32)],
-        rank, pair_low, row_points, point_factor,
-    )
-
-
-PACKED = (NSECT, 2 * GROUPS, LANES)
+        pair_low, row_points, point_factor,
+    )
+
+
 LINES = NSECT * 2 * GROUPS
 
 
@@ -371,12 +404,12 @@
     return run(
         synth_kernel,
         "synth",
-        struct(PACKED, BF16),
+        struct((LINES, LANES), BF16),
         [whole()] * 6,
         [
             vmem((LANES, LANES), F32),
             vmem((LANES, LANES), F32),
-            vmem((10 * NSECT, LANES), BF16),
+            vmem((2 * MOST * NSECT, LANES), BF16),
             vmem((LINES, LANES), F32),
         ],
         block, coarse, fine, trig, slots, scale,
@@ -387,21 +420,21 @@
     return run(
         tendency_kernel,
         "tendency",
-        struct(PACKED, BF16),
+        struct((LINES, LANES), BF16),
         [whole()] * 3,
         [vmem((LINES, LANES), F32)],
         grid, couple, pf,
     )
 
 
-def expand(rank, row_points, grid):
+def expand(row_points, grid):
     return run(
         expand_kernel,
         "expand",
         struct((2, NSECT, ROWS * SECW), BF16),
-        [scalars(), scalars(), whole()],
+        [scalars(), whole()],
         [vmem((LINES, LANES), F32), vmem((NSECT, 13 * LANES), F32)],
-        rank, row_points, grid,
+        row_points, grid,
     )
 
 
@@ -413,7 +446,7 @@
         [whole()] * 6,
         [
             vmem((LINES, LANES), F32),
-            vmem((10 * NSECT, LANES), BF16),
+            vmem((2 * MOST * NSECT, LANES), BF16),
             vmem((LANES, LANES), F32),
             vmem((LANES, LANES), F32),
         ],
@@ -421,25 +454,31 @@
     )
 
 
-def to_bands(rank, pair_low, spec, legendre):
+def to_bands(pair_low, spec, legendre):
     return run(
         legendre_kernel,
         "legendre",
         struct((BANDS, 8, LANES), BF16),
-        [scalars(), scalars(), whole(), whole()],
-        [vmem((16, 6 * LANES), F32)],
-        rank, pair_low, spec, legendre,
-    )
-
-
-def project(rank, pair_low, back, gauss_weight, legendre):
+        [scalars(), in_hbm(), in_hbm()],
+        [
+            vmem((16, 6 * LANES), F32),
+            vmem((2, 2, NMAX), BF16),
+            vmem((2, NMAX, NMAX), BF16),
+            pltpu.SemaphoreType.DMA((5,)),
+        ],
+        pair_low, spec, legendre,
+        grant=FULL_GRANT,
+    )
+
+
+def project(pair_low, back, gauss_weight, legendre):
     return run(
         project_kernel,
         "project",
         struct((4, 1, NMAX), F32),
-        [scalars(), scalars(), whole(), whole(), whole()],
+        [scalars(), whole(), whole(), whole()],
         [vmem((16, NMAX), F32)],
-        rank, pair_low, back, gauss_weight[None, :], legendre,
+        pair_low, back, gauss_weight[None, :], legendre,
     )
 
 
@@ -489,31 +528,33 @@
 
 
 def rows_fit(row_points):
-    width = ((row_points + NSECT - 1) // NSECT).reshape(BANDS, 5, GROUPS)
-    total = width[:, 0] + width[:, 1, ::-1] + width[:, 2] + width[:, 3, ::-1] + width[:, 4]
+    width = ((row_points + NSECT - 1) // NSECT).reshape(BANDS, ROWS)
+    member = jnp.array([[row in rows for row in range(ROWS)] for rows in GROUP_ROWS])
+    total = jnp.sum(jnp.where(member[None], width[:, None], 0), axis=2)
     return jnp.max(total) <= LANES
 
 
 def per_device(spec_in, pair_low, row_points, legendre, gauss_weight, couple, point_factor):
     rank = lax.axis_index(WAVE).astype(jnp.int32).reshape(1)
-    outgoing = to_bands(rank, pair_low, spec_in[:, :, 0], legendre)
+    outgoing = to_bands(pair_low, spec_in[:, :, 0], legendre)
     block = lax.all_to_all(outgoing, WAVE, split_axis=0, concat_axis=0, tiled=True)
-    coarse, fine, trig, slots, pf, scale = make_tables(rank, pair_low, row_points, point_factor)
+    coarse, fine, trig, slots, pf, scale = make_tables(pair_low, row_points, point_factor)
 
     def cross(x):
-        return lax.all_to_all(x, "sect", split_axis=0, concat_axis=0, tiled=True)
+        x = x.reshape(NSECT, GROUPS, 2, LANES)
+        return lax.all_to_all(x, "sect", split_axis=0, concat_axis=0, tiled=True).reshape(LINES, LANES)
 
     def packed_path(block):
         grid = cross(synthesize(block, coarse, fine, trig, slots, scale))
         received = cross(tend_of(grid, couple, pf))
-        return expand(rank, row_points, grid), analyse(received, coarse, fine, trig, slots, scale)
+        return expand(row_points, grid), analyse(received, coarse, fine, trig, slots, scale)
 
     def every_slot(block):
         return loose_path(block, rank, pair_low, row_points, couple, point_factor)
 
     grid_field, analysis = lax.cond(rows_fit(row_points), packed_path, every_slot, block)
     back = lax.all_to_all(analysis, WAVE, split_axis=0, concat_axis=0, tiled=True)
-    spec_out = project(rank, pair_low, back, gauss_weight, legendre)
+    spec_out = project(pair_low, back, gauss_weight, legendre)
     return grid_field[:, :, None, :], spec_out.reshape(2, 2, 1, NMAX)
 
 

time: 110 us -> 106 us (0.964)
  local copies, waits for them, and re-layouts: 2.48 us -> 0.13 us
  blocking collectives: 32.8 us -> 31.2 us
    unnamed x16 -> x14, local copies, waits for them, and re-layouts: 2.15 us -> 0.03 us
    all_to_all x1, blocking collectives: 32.8 us -> 31.2 us  [cross(): lax.all_to_all(x, 'sect', split_axis=0, concat_axis=0, tiled=True)]
where the time goes in v3:
time: 106 us; the launch traced here: 105 us
  blocking collectives  31.2 us (29%)
  starting transfers between devices  31.1 us (29%)
  waiting for transfers between devices  26.9 us (25%)
  Pallas kernels  13.9 us (13%)
  between operations  1.39 us (1%)
    all_to_all x1, blocking collectives, cross(): lax.all_to_all(x, 'sect', split_axis=0, concat_axis=0, tiled=True)  31.2 us
    all_to_all x1, starting transfers between devices, per_device(): lax.all_to_all(outgoing, WAVE, split_axis=0, concat_axis=0, tiled=True)  17.4 us
    all_to_all x1, waiting for transfers between devices, cross(): lax.all_to_all(x, 'sect', split_axis=0, concat_axis=0, tiled=True)  15.9 us
    pallas_call x7, Pallas kernels, run(): pl.pallas_call(kernel, out_shape=outs, in_specs=in_specs, out_specs=[whol...  13.9 us
    all_to_all x1, waiting for transfers between devices, per_device(): lax.all_to_all(analysis, WAVE, split_axis=0, concat_axis=0, tiled=True)  7.37 us
    all_to_all x1, starting transfers between devices, cross(): lax.all_to_all(x, 'sect', split_axis=0, concat_axis=0, tiled=True)  7.29 us
    all_to_all x1, starting transfers between devices, per_device(): lax.all_to_all(analysis, WAVE, split_axis=0, concat_axis=0, tiled=True)  6.35 us
    all_to_all x1, waiting for transfers between devices, per_device(): lax.all_to_all(outgoing, WAVE, split_axis=0, concat_axis=0, tiled=True)  3.64 us
  transfers between devices with their start and end apart: 3, of which 3 were waited for; matrix products, arithmetic and copies ran while one was open for 1% of the time, Pallas kernels for 4%

profile of v3, /device:TPU:1, one launch (start us, length us, event | category | flops | bytes accessed | tf_op | source)
XLA Modules:
  0.0 105.4 jit_solution(104679797853514580)
XLA Ops:
  0.6 0.0 copy-start.11
  0.6 0.0 copy-start.9
  0.7 0.0 copy-start.8
  0.7 0.0 copy-start.7
  0.7 0.0 copy-start.6
  0.7 3.2 %legendre.1 = bf16[16,8,128]{2,1,0:T(8,128)(2,1)} custom-call(s32[32]{0:T(128)} %low_ref.5, bf16[2,2,640]{2,1,0:T(2,128)(2,1)} %bitcast.64, bf16[2,640,640]{2,1,0:T(8,128)(2,1)} %leg_ref.1), custom_call_target="tpu_custom_call" | custom-call | tf_op jit(solution)/shard_map/legendre/pallas_call | solution.py:363
  3.8 17.4 %all-to-all-start.4 = ((bf16[16,8,128]{2,1,0:T(8,128)(2,1)}), bf16[16,8,128]{2,1,0:T(8,128)(2,1)S(1)}, u32[]{:S(2)}, u32[]{:S(2)}) async-start(bf16[16,8,128]{2,1,0:T(8,128)(2,1)} %legendre.1), calls=%async_computation.4 | async-start | bytes 65536 | tf_op jit(solution)/shard_map/all_to_all | solution.py:540
  21.3 0.0 copy-done.8
  21.3 0.0 copy-done.9
  21.3 0.0 copy-done.7
  21.3 2.2 %tables.1 = (f32[2,40,8,128]{3,2,1,0:T(8,128)}, f32[2,40,8,128]{3,2,1,0:T(8,128)}, bf16[7,128,128]{2,1,0:T(8,128)(2,1)}, s32[3,7,128]{2,1,0:T(8,128)S(1)}, f32[2...) custom-call(s32[32]{0:T(128)S(1)} %copy-done.9, s32[640]{0:T(1024)S(1)} %copy-done.8, f32[2,1,1640]{2,1,0:T(1,128)S(1)} %copy-done.7), custom_call_target="tpu_custom_call" | custom-call | tf_op jit(solution)/shard_map/tables/pallas_call | solution.py:363
  23.5 0.1 broadcast_in_dim.90
  23.6 0.2 select_reduce_fusion
  23.8 0.6 reduce_max.9
  25.1 3.6 %all-to-all-done.4 = bf16[16,8,128]{2,1,0:T(8,128)(2,1)S(1)} async-done(((bf16[16,8,128]{2,1,0:T(8,128)(2,1)}), bf16[16,8,128]{2,1,0:T(8,128)(2,1)S(1)}, u32[]{:S(2)}, u32[]{:S(2)}) %all-to-all-start.4) | async-done | bytes 32800 | tf_op jit(solution)/shard_map/all_to_all | solution.py:540
  28.7 61.2 %conditional.1 = (bf16[16,8,128]{2,1,0:T(8,128)(2,1)}, bf16[2,64,1,1640]{3,1,2,0:T(8,128)(2,1)}) conditional(s32[]{:T(128)} %convert_element_type.54, (s32[32]{0:T(128)S(1)}, s32[]{:T(128)}, s32[]{:T(128)}, s32[640]{0:T(1024)S(1)}, bf16[16,8,128]{2,1,0:T(8,128)(2,1)S(1)}, /*index=5*/bf16[64,64]{1,0:T(8,128)(2,1)S(1)}, ...), branch_computations={%region_2.5_spmd, %region_5.6_spmd} | conditional | flops 151992576 | bytes 32076354 | solution.py:555
  28.8 2.3 %synth.1 = bf16[896,128]{1,0:T(8,128)(2,1)S(1)} custom-call(bf16[16,8,128]{2,1,0:T(8,128)(2,1)S(1)} %get-tuple-element.43.block_ref, f32[2,40,8,128]{3,2,1,0:T(8,128)} %get-tuple-element.44.coarse_ref, f32[2,40,8,128]{3,2,1,0:T(8,128)} %get-tuple-element.45.fine_ref, bf16[7,128,128]{2,1,0:T(8,128)(2,1)} %get-tuple-element.46.trig_ref, ...), custom_call_target="tpu_custom_call" | custom-call | tf_op jit(solution)/shard_map/cond/branch_1_fun/synth/pallas_call | solution.py:363
  31.0 0.0 copy-start.3
  31.0 0.0 copy-start.4
  31.0 0.0 copy-start.5
  31.1 31.2 %all_to_all.26 = bf16[64,7,2,128]{3,2,1,0:T(2,128)(2,1)S(1)} all-to-all(bf16[64,7,2,128]{3,2,1,0:T(2,128)(2,1)S(1)} %bitcast.53), channel_id=1, replica_groups=mesh['wave_0'=8,'wave_1'=2,'sect'=64] {'sect'}, dimensions={0} | all-to-all | bytes 458752 | tf_op jit(solution)/shard_map/cond/branch_1_fun/all_to_all | solution.py:545
  62.3 1.0 tendency.1
  63.3 7.3 %all-to-all-start.1 = ((bf16[64,7,2,128]{3,2,1,0:T(2,128)(2,1)}), bf16[64,7,2,128]{3,2,1,0:T(2,128)(2,1)S(1)}, u32[]{:S(2)}, u32[]{:S(2)}) async-start(bf16[64,7,2,128]{3,2,1,0:T(2,128)(2,1)} %bitcast.24), calls=%async_computation.1 | async-start | bytes 458752 | tf_op jit(solution)/shard_map/cond/branch_1_fun/all_to_all | solution.py:545
  70.6 1.9 %expand.1 = bf16[2,64,1640]{2,1,0:T(8,128)(2,1)} custom-call(s32[640]{0:T(1024)S(1)} %get-tuple-element.51.points_ref, bf16[896,128]{1,0:T(8,128)(2,1)S(1)} %bitcast.51), custom_call_target="tpu_custom_call" | custom-call | tf_op jit(solution)/shard_map/cond/branch_1_fun/expand/pallas_call | solution.py:363
  72.4 15.9 %all-to-all-done.1 = bf16[64,7,2,128]{3,2,1,0:T(2,128)(2,1)S(1)} async-done(((bf16[64,7,2,128]{3,2,1,0:T(2,128)(2,1)}), bf16[64,7,2,128]{3,2,1,0:T(2,128)(2,1)S(1)}, u32[]{:S(2)}, u32[]{:S(2)}) %all-to-all-start.1) | async-done | bytes 229408 | tf_op jit(solution)/shard_map/cond/branch_1_fun/all_to_all | solution.py:545
  88.3 0.0 copy-done.4
  88.3 1.7 %analysis.1 = bf16[16,8,128]{2,1,0:T(8,128)(2,1)} custom-call(bf16[896,128]{1,0:T(8,128)(2,1)S(1)} %bitcast.52, f32[2,40,8,128]{3,2,1,0:T(8,128)S(1)} %copy-done.3, f32[2,40,8,128]{3,2,1,0:T(8,128)S(1)} %copy-done.4, bf16[7,128,128]{2,1,0:T(8,128)(2,1)S(1)} %copy-done.5, s32[3,7,128]{2,1,0:T(8,128)S(1)} %get-tuple-element.47.slot_ref, ...), custom_call_target="tpu_custom_call" | custom-call | tf_op jit(solution)/shard_map/cond/branch_1_fun/analysis/pallas_call | solution.py:363
  90.0 6.4 %all-to-all-start.5 = ((bf16[16,8,128]{2,1,0:T(8,128)(2,1)}), bf16[16,8,128]{2,1,0:T(8,128)(2,1)S(1)}, u32[]{:S(2)}, u32[]{:S(2)}) async-start(bf16[16,8,128]{2,1,0:T(8,128)(2,1)} %get-tuple-element.69), calls=%async_computation.5 | async-start | bytes 65536 | tf_op jit(solution)/shard_map/all_to_all | solution.py:556
  96.3 0.0 copy-done.10
  96.3 7.4 %all-to-all-done.5.back_ref = bf16[16,8,128]{2,1,0:T(8,128)(2,1)S(1)} async-done(((bf16[16,8,128]{2,1,0:T(8,128)(2,1)}), bf16[16,8,128]{2,1,0:T(8,128)(2,1)S(1)}, u32[]{:S(2)}, u32[]{:S(2)}) %all-to-all-start.5) | async-done | bytes 32800 | tf_op jit(solution)/shard_map/all_to_all | solution.py:556
  103.7 0.0 copy-done
  103.7 1.7 %project.1 = f32[4,1,640]{2,1,0:T(1,128)} custom-call(s32[32]{0:T(128)S(1)} %copy-done.9, bf16[16,8,128]{2,1,0:T(8,128)(2,1)S(1)} %all-to-all-done.5.back_ref, f32[1,640]{1,0:T(1,128)S(1)} %broadcast_in_dim.93.gauss_ref, bf16[2,640,640]{2,1,0:T(8,128)(2,1)S(1)} %copy-done), custom_call_target="tpu_custom_call" | custom-call | tf_op jit(solution)/shard_map/project/pallas_call | solution.py:363
  (8 shorter events, 0.0 us)
Async XLA Ops:
  0.6 23.0 %copy-start.11 = (pred[7,40]{1,0:T(8,128)(4,1)S(1)}, pred[7,40]{1,0:T(8,128)(4,1)}, u32[]{:S(2)}) copy-start(pred[7,40]{1,0:T(8,128)(4,1)} %constant.123.clone) | copy-start | bytes 844
  0.6 20.6 %copy-start.9 = (s32[32]{0:T(128)S(1)}, s32[32]{0:T(128)}, u32[]{:S(2)}) copy-start(s32[32]{0:T(128)} %low_ref.5) | copy-start | bytes 388
  0.7 20.6 %copy-start.8 = (s32[640]{0:T(1024)S(1)}, s32[640]{0:T(1024)}, u32[]{:S(2)}) copy-start(s32[640]{0:T(1024)} %points_ref.1) | copy-start | bytes 7684
  0.7 20.6 %copy-start.7 = (f32[2,1,1640]{2,1,0:T(1,128)S(1)}, f32[2,1,1640]{2,1,0:T(1,128)}, u32[]{:S(2)}) copy-start(f32[2,1,1640]{2,1,0:T(1,128)} %factor_ref.1) | copy-start | bytes 39364
  0.7 28.1 %copy-start.6 = (bf16[64,64]{1,0:T(8,128)(2,1)S(1)}, bf16[64,64]{1,0:T(8,128)(2,1)}, u32[]{:S(2)}) copy-start(bf16[64,64]{1,0:T(8,128)(2,1)} %param.15) | copy-start | bytes 24580
  3.8 24.9 %all-to-all-start.4 = ((bf16[16,8,128]{2,1,0:T(8,128)(2,1)}), bf16[16,8,128]{2,1,0:T(8,128)(2,1)S(1)}, u32[]{:S(2)}, u32[]{:S(2)}) async-start(bf16[16,8,128]{2,1,0:T(8,128)(2,1)} %legendre.1), calls=%async_computation.4 | async-start | bytes 65536 | tf_op jit(solution)/shard_map/all_to_all | solution.py:540
  28.7 67.6 %copy-start.10 = (f32[640]{0:T(1024)S(1)}, f32[640]{0:T(1024)}, u32[]{:S(2)}) copy-start(f32[640]{0:T(1024)} %param.14) | copy-start | bytes 7684
  28.7 75.0 %copy-start = (bf16[2,640,640]{2,1,0:T(8,128)(2,1)S(1)}, bf16[2,640,640]{2,1,0:T(8,128)(2,1)}, u32[]{:S(2)}) copy-start(bf16[2,640,640]{2,1,0:T(8,128)(2,1)} %leg_ref.1) | copy-start | bytes 4915204
  31.0 57.3 %copy-start.3 = (f32[2,40,8,128]{3,2,1,0:T(8,128)S(1)}, f32[2,40,8,128]{3,2,1,0:T(8,128)}, u32[]{:S(2)}) copy-start(f32[2,40,8,128]{3,2,1,0:T(8,128)} %get-tuple-element.44.coarse_ref) | copy-start | bytes 983044 | tf_op jit(solution)/shard_map/cond
  31.0 57.3 %copy-start.4 = (f32[2,40,8,128]{3,2,1,0:T(8,128)S(1)}, f32[2,40,8,128]{3,2,1,0:T(8,128)}, u32[]{:S(2)}) copy-start(f32[2,40,8,128]{3,2,1,0:T(8,128)} %get-tuple-element.45.fine_ref) | copy-start | bytes 983044 | tf_op jit(solution)/shard_map/cond
  31.0 57.3 %copy-start.5 = (bf16[7,128,128]{2,1,0:T(8,128)(2,1)S(1)}, bf16[7,128,128]{2,1,0:T(8,128)(2,1)}, u32[]{:S(2)}) copy-start(bf16[7,128,128]{2,1,0:T(8,128)(2,1)} %get-tuple-element.46.trig_ref) | copy-start | bytes 688132 | tf_op jit(solution)/shard_map/cond
  63.3 25.0 %all-to-all-start.1 = ((bf16[64,7,2,128]{3,2,1,0:T(2,128)(2,1)}), bf16[64,7,2,128]{3,2,1,0:T(2,128)(2,1)S(1)}, u32[]{:S(2)}, u32[]{:S(2)}) async-start(bf16[64,7,2,128]{3,2,1,0:T(2,128)(2,1)} %bitcast.24), calls=%async_computation.1 | async-start | bytes 458752 | tf_op jit(solution)/shard_map/cond/branch_1_fun/all_to_all | solution.py:545
  90.0 13.7 %all-to-all-start.5 = ((bf16[16,8,128]{2,1,0:T(8,128)(2,1)}), bf16[16,8,128]{2,1,0:T(8,128)(2,1)S(1)}, u32[]{:S(2)}, u32[]{:S(2)}) async-start(bf16[16,8,128]{2,1,0:T(8,128)(2,1)} %get-tuple-element.69), calls=%async_computation.5 | async-start | bytes 65536 | tf_op jit(solution)/shard_map/all_to_all | solution.py:556

commit v4 on v3

--- a/solution.py
+++ b/solution.py
@@ -87,8 +87,12 @@
     return found
 
 
-def tables_kernel(low_ref, points_ref, factor_ref, coarse_ref, fine_ref, trig_ref, slot_ref, pf_ref, scale_ref, pad_ref):
-    first = wave_rank() * ROWS
+def tables_kernel(low_ref, points_ref, factor_ref, coarse_ref, fine_ref, trig_ref, slot_ref, pf_ref, scale_ref, pick_ref, pad_ref):
+    rank = wave_rank()
+    first = rank * ROWS
+    for p in range(2):
+        leading, odd = slot_signs(low_ref[2 * rank + p], (1, NMAX))
+        pick_ref[p : p + 1, :] = jnp.where(leading, 0, 2) + jnp.where(odd, 4, 0)
     waves = wave_lanes(low_ref, (8, LANES))
     waves_f = waves.astype(F32)
     wave_row = waves_f[0:1]
@@ -267,10 +271,12 @@
     return leading, odd
 
 
-def legendre_kernel(low_ref, spec_hbm, leg_hbm, out_ref, wide_ref, spec_ref, leg_ref, sems):
-    half = NMAX // 2
+def legendre_kernel(low_hbm, spec_hbm, leg_hbm, out_ref, wide_ref, low_ref, spec_ref, leg_ref, sems):
+    low_copy = pltpu.make_async_copy(low_hbm, low_ref, sems.at[5])
+    low_copy.start()
     spec_copy = pltpu.make_async_copy(spec_hbm, spec_ref, sems.at[4])
     spec_copy.start()
+    half = NMAX // 2
     leg_copies = []
     for p in range(2):
         for part in range(2):
@@ -280,22 +286,25 @@
             )
             leg_copies[-1].start()
     wide_ref[...] = jnp.zeros((16, 6 * LANES), F32)
-    spec_copy.wait()
     line = lax.broadcasted_iota(jnp.int32, (8, NMAX), 0)
     h = line >> 2
     member = (line >> 1) & 1
     part = line & 1
-    found = []
+    spec_copy.wait()
+    low_copy.wait()
+    values = []
     for p in range(2):
         low = low_ref[2 * wave_rank() + p]
         leading, odd = slot_signs(low, (8, NMAX))
         spec = spec_ref[p].astype(F32)
         value = jnp.where(part == 0, spec[0:1], spec[1:2])
         value = jnp.where((member == 0) == leading, value, 0.0)
-        value = jnp.where((h == 1) & odd, -value, value)
+        values.append(jnp.where((h == 1) & odd, -value, value).astype(BF16))
+    found = []
+    for p in range(2):
         leg_copies[2 * p].wait()
         leg_copies[2 * p + 1].wait()
-        found.append(jnp.dot(value.astype(BF16), leg_ref[p], preferred_element_type=F32))
+        found.append(jnp.dot(values[p], leg_ref[p], preferred_element_type=F32))
     upper = line < 4
     wide_ref[0:8, 0:NMAX] = jnp.where(upper, found[0], pltpu.roll(found[1], 4, axis=0))
     wide_ref[8:16, 0:NMAX] = jnp.where(upper, pltpu.roll(found[0], 4, axis=0), found[1])
@@ -309,7 +318,7 @@
         out_ref[band] = jnp.where(lane < 64, north, south).astype(BF16)
 
 
-def project_kernel(low_ref, back_ref, gauss_ref, leg_ref, out_ref, wide_ref):
+def project_kernel(pick_ref, back_ref, gauss_ref, leg_ref, out_ref, wide_ref):
     lane = lane_iota((8, LANES))
     for tile in range(NMAX // LANES):
         north = jnp.zeros((8, LANES), F32)
@@ -335,15 +344,15 @@
         jnp.where(upper, pltpu.roll(both, 4, axis=0), less),
     ]
     for p in range(2):
-        low = low_ref[2 * wave_rank() + p]
-        leading, odd = slot_signs(low, (1, NMAX))
+        pick = pick_ref[p : p + 1, :]
         product = lax.dot_general(
             forms[p].astype(BF16), leg_ref[p], (((1,), (1,)), ((), ())), preferred_element_type=F32
         )
         for r in range(2):
-            lower = jnp.where(odd, product[4 + r : 5 + r], product[r : r + 1])
-            higher = jnp.where(odd, product[6 + r : 7 + r], product[2 + r : 3 + r])
-            out_ref[2 * p + r] = jnp.where(leading, lower, higher)
+            chosen = product[r : r + 1]
+            for first in (2, 4, 6):
+                chosen = jnp.where(pick == first, product[first + r : first + r + 1], chosen)
+            out_ref[2 * p + r] = chosen
 
 
 def whole():
@@ -390,6 +399,7 @@
             struct((3, GROUPS, LANES), jnp.int32),
             struct((2, GROUPS, LANES), F32),
             struct((LANES, LANES), F32),
+            struct((2, NMAX), jnp.int32),
         ],
         [scalars(), scalars(), whole()],
         [vmem((8, 14 * LANES), F32)],
@@ -459,26 +469,27 @@
         legendre_kernel,
         "legendre",
         struct((BANDS, 8, LANES), BF16),
-        [scalars(), in_hbm(), in_hbm()],
+        [in_hbm(), in_hbm(), in_hbm()],
         [
             vmem((16, 6 * LANES), F32),
+            SMEM((32,), jnp.int32),
             vmem((2, 2, NMAX), BF16),
             vmem((2, NMAX, NMAX), BF16),
-            pltpu.SemaphoreType.DMA((5,)),
+            pltpu.SemaphoreType.DMA((6,)),
         ],
         pair_low, spec, legendre,
         grant=FULL_GRANT,
     )
 
 
-def project(pair_low, back, gauss_weight, legendre):
+def project(pick, back, gauss_weight, legendre):
     return run(
         project_kernel,
         "project",
         struct((4, 1, NMAX), F32),
-        [scalars(), whole(), whole(), whole()],
+        [whole()] * 4,
         [vmem((16, NMAX), F32)],
-        pair_low, back, gauss_weight[None, :], legendre,
+        pick, back, gauss_weight[None, :], legendre,
     )
 
 
@@ -538,7 +549,7 @@
     rank = lax.axis_index(WAVE).astype(jnp.int32).reshape(1)
     outgoing = to_bands(pair_low, spec_in[:, :, 0], legendre)
     block = lax.all_to_all(outgoing, WAVE, split_axis=0, concat_axis=0, tiled=True)
-    coarse, fine, trig, slots, pf, scale = make_tables(pair_low, row_points, point_factor)
+    coarse, fine, trig, slots, pf, scale, pick = make_tables(pair_low, row_points, point_factor)
 
     def cross(x):
         x = x.reshape(NSECT, GROUPS, 2, LANES)
@@ -554,7 +565,7 @@
 
     grid_field, analysis = lax.cond(rows_fit(row_points), packed_path, every_slot, block)
     back = lax.all_to_all(analysis, WAVE, split_axis=0, concat_axis=0, tiled=True)
-    spec_out = project(pair_low, back, gauss_weight, legendre)
+    spec_out = project(pick, back, gauss_weight, legendre)
     return grid_field[:, :, None, :], spec_out.reshape(2, 2, 1, NMAX)
 
 

time: 106 us -> 105 us (level)
  Pallas kernels: 13.9 us -> 12.6 us
    pallas_call x7, Pallas kernels: 13.9 us -> 12.6 us  [run(): pl.pallas_call(kernel, out_shape=outs, in_specs=in_specs, out_specs=[whol...]
where the time goes in v4:
time: 105 us; the launch traced here: 104 us
  blocking collectives  31.2 us (30%)
  starting transfers between devices  31.1 us (30%)
  waiting for transfers between devices  26.9 us (26%)
  Pallas kernels  12.6 us (12%)
  between operations  1.39 us (1%)
    all_to_all x1, blocking collectives, cross(): lax.all_to_all(x, 'sect', split_axis=0, concat_axis=0, tiled=True)  31.2 us
    all_to_all x1, starting transfers between devices, per_device(): lax.all_to_all(outgoing, WAVE, split_axis=0, concat_axis=0, tiled=True)  17.4 us
    all_to_all x1, waiting for transfers between devices, cross(): lax.all_to_all(x, 'sect', split_axis=0, concat_axis=0, tiled=True)  15.9 us
    pallas_call x7, Pallas kernels, run(): pl.pallas_call(kernel, out_shape=outs, in_specs=in_specs, out_specs=[whol...  12.6 us
    all_to_all x1, waiting for transfers between devices, per_device(): lax.all_to_all(analysis, WAVE, split_axis=0, concat_axis=0, tiled=True)  7.37 us
    all_to_all x1, starting transfers between devices, cross(): lax.all_to_all(x, 'sect', split_axis=0, concat_axis=0, tiled=True)  7.29 us
    all_to_all x1, starting transfers between devices, per_device(): lax.all_to_all(analysis, WAVE, split_axis=0, concat_axis=0, tiled=True)  6.37 us
    all_to_all x1, waiting for transfers between devices, per_device(): lax.all_to_all(outgoing, WAVE, split_axis=0, concat_axis=0, tiled=True)  3.63 us
  transfers between devices with their start and end apart: 3, of which 3 were waited for; matrix products, arithmetic and copies ran while one was open for 1% of the time, Pallas kernels for 4%

profile of v4, /device:TPU:1, one launch (start us, length us, event | category | flops | bytes accessed | tf_op | source)
XLA Modules:
  0.0 104.2 jit_solution(2077053038911354960)
XLA Ops:
  0.6 0.0 copy-start.11
  0.6 0.0 copy-start.9
  0.7 0.0 copy-start.8
  0.7 0.0 copy-start.7
  0.7 0.0 copy-start.6
  0.7 2.4 %legendre.1 = bf16[16,8,128]{2,1,0:T(8,128)(2,1)} custom-call(s32[32]{0:T(128)} %low_ref.1, bf16[2,2,640]{2,1,0:T(2,128)(2,1)} %bitcast.63, bf16[2,640,640]{2,1,0:T(8,128)(2,1)} %leg_ref.1), custom_call_target="tpu_custom_call" | custom-call | tf_op jit(solution)/shard_map/legendre/pallas_call | solution.py:372
  3.1 17.4 %all-to-all-start.4 = ((bf16[16,8,128]{2,1,0:T(8,128)(2,1)}), bf16[16,8,128]{2,1,0:T(8,128)(2,1)S(1)}, u32[]{:S(2)}, u32[]{:S(2)}) async-start(bf16[16,8,128]{2,1,0:T(8,128)(2,1)} %legendre.1), calls=%async_computation.4 | async-start | bytes 65536 | tf_op jit(solution)/shard_map/all_to_all | solution.py:551
  20.5 0.0 copy-done.8
  20.5 0.0 copy-done.9
  20.5 0.0 copy-done.7
  20.5 2.2 %tables.1 = (f32[2,40,8,128]{3,2,1,0:T(8,128)}, f32[2,40,8,128]{3,2,1,0:T(8,128)}, bf16[7,128,128]{2,1,0:T(8,128)(2,1)}, s32[3,7,128]{2,1,0:T(8,128)S(1)}, f32[2...) custom-call(s32[32]{0:T(128)S(1)} %copy-done.9, s32[640]{0:T(1024)S(1)} %copy-done.8, ...), custom_call_target="tpu_custom_call" | custom-call | tf_op jit(solution)/shard_map/tables/pallas_call | solution.py:372
  22.7 0.1 broadcast_in_dim.90
  22.8 0.0 copy-done.11
  22.8 0.2 select_reduce_fusion
  23.0 0.6 reduce_max.9
  24.3 3.6 %all-to-all-done.4 = bf16[16,8,128]{2,1,0:T(8,128)(2,1)S(1)} async-done(((bf16[16,8,128]{2,1,0:T(8,128)(2,1)}), bf16[16,8,128]{2,1,0:T(8,128)(2,1)S(1)}, u32[]{:S(2)}, u32[]{:S(2)}) %all-to-all-start.4) | async-done | bytes 32800 | tf_op jit(solution)/shard_map/all_to_all | solution.py:551
  28.0 61.3 %conditional.1 = (bf16[16,8,128]{2,1,0:T(8,128)(2,1)}, bf16[2,64,1,1640]{3,1,2,0:T(8,128)(2,1)}) conditional(s32[]{:T(128)} %convert_element_type.54, (s32[32]{0:T(128)S(1)}, s32[]{:T(128)}, s32[]{:T(128)}, s32[640]{0:T(1024)S(1)}, bf16[16,8,128]{2,1,0:T(8,128)(2,1)S(1)}, /*index=5*/bf16[64,64]{1,0:T(8,128)(2,1)S(1)}, ...), branch_computations={%region_2.5_spmd, %region_5.6_spmd} | conditional | flops 151992576 | bytes 32076354 | solution.py:566
  28.0 2.3 %synth.1 = bf16[896,128]{1,0:T(8,128)(2,1)S(1)} custom-call(bf16[16,8,128]{2,1,0:T(8,128)(2,1)S(1)} %get-tuple-element.43.block_ref, f32[2,40,8,128]{3,2,1,0:T(8,128)} %get-tuple-element.44.coarse_ref, f32[2,40,8,128]{3,2,1,0:T(8,128)} %get-tuple-element.45.fine_ref, bf16[7,128,128]{2,1,0:T(8,128)(2,1)} %get-tuple-element.46.trig_ref, ...), custom_call_target="tpu_custom_call" | custom-call | tf_op jit(solution)/shard_map/cond/branch_1_fun/synth/pallas_call | solution.py:372
  30.3 0.0 copy-start.3
  30.3 0.0 copy-start.4
  30.3 0.0 copy-start.5
  30.3 31.2 %all_to_all.26 = bf16[64,7,2,128]{3,2,1,0:T(2,128)(2,1)S(1)} all-to-all(bf16[64,7,2,128]{3,2,1,0:T(2,128)(2,1)S(1)} %bitcast.53), channel_id=1, replica_groups=mesh['wave_0'=8,'wave_1'=2,'sect'=64] {'sect'}, dimensions={0} | all-to-all | bytes 458752 | tf_op jit(solution)/shard_map/cond/branch_1_fun/all_to_all | solution.py:556
  61.5 1.0 tendency.1
  62.5 7.3 %all-to-all-start.1 = ((bf16[64,7,2,128]{3,2,1,0:T(2,128)(2,1)}), bf16[64,7,2,128]{3,2,1,0:T(2,128)(2,1)S(1)}, u32[]{:S(2)}, u32[]{:S(2)}) async-start(bf16[64,7,2,128]{3,2,1,0:T(2,128)(2,1)} %bitcast.24), calls=%async_computation.1 | async-start | bytes 458752 | tf_op jit(solution)/shard_map/cond/branch_1_fun/all_to_all | solution.py:556
  69.8 1.9 %expand.1 = bf16[2,64,1640]{2,1,0:T(8,128)(2,1)} custom-call(s32[640]{0:T(1024)S(1)} %get-tuple-element.51.points_ref, bf16[896,128]{1,0:T(8,128)(2,1)S(1)} %bitcast.51), custom_call_target="tpu_custom_call" | custom-call | tf_op jit(solution)/shard_map/cond/branch_1_fun/expand/pallas_call | solution.py:372
  71.7 15.9 %all-to-all-done.1 = bf16[64,7,2,128]{3,2,1,0:T(2,128)(2,1)S(1)} async-done(((bf16[64,7,2,128]{3,2,1,0:T(2,128)(2,1)}), bf16[64,7,2,128]{3,2,1,0:T(2,128)(2,1)S(1)}, u32[]{:S(2)}, u32[]{:S(2)}) %all-to-all-start.1) | async-done | bytes 229408 | tf_op jit(solution)/shard_map/cond/branch_1_fun/all_to_all | solution.py:556
  87.5 0.0 copy-done.3
  87.5 0.0 copy-done.5
  87.5 1.7 %analysis.1 = bf16[16,8,128]{2,1,0:T(8,128)(2,1)} custom-call(bf16[896,128]{1,0:T(8,128)(2,1)S(1)} %bitcast.52, f32[2,40,8,128]{3,2,1,0:T(8,128)S(1)} %copy-done.3, f32[2,40,8,128]{3,2,1,0:T(8,128)S(1)} %copy-done.4, bf16[7,128,128]{2,1,0:T(8,128)(2,1)S(1)} %copy-done.5, s32[3,7,128]{2,1,0:T(8,128)S(1)} %get-tuple-element.47.slot_ref, ...), custom_call_target="tpu_custom_call" | custom-call | tf_op jit(solution)/shard_map/cond/branch_1_fun/analysis/pallas_call | solution.py:372
  89.3 6.4 %all-to-all-start.5 = ((bf16[16,8,128]{2,1,0:T(8,128)(2,1)}), bf16[16,8,128]{2,1,0:T(8,128)(2,1)S(1)}, u32[]{:S(2)}, u32[]{:S(2)}) async-start(bf16[16,8,128]{2,1,0:T(8,128)(2,1)} %get-tuple-element.71), calls=%async_computation.5 | async-start | bytes 65536 | tf_op jit(solution)/shard_map/all_to_all | solution.py:567
  95.6 7.4 %all-to-all-done.5.back_ref = bf16[16,8,128]{2,1,0:T(8,128)(2,1)S(1)} async-done(((bf16[16,8,128]{2,1,0:T(8,128)(2,1)}), bf16[16,8,128]{2,1,0:T(8,128)(2,1)S(1)}, u32[]{:S(2)}, u32[]{:S(2)}) %all-to-all-start.5) | async-done | bytes 32800 | tf_op jit(solution)/shard_map/all_to_all | solution.py:567
  103.0 1.2 %project.1 = f32[4,1,640]{2,1,0:T(1,128)} custom-call(s32[2,640]{1,0:T(2,128)S(1)} %get-tuple-element.70.pick_ref, bf16[16,8,128]{2,1,0:T(8,128)(2,1)S(1)} %all-to-all-done.5.back_ref, f32[1,640]{1,0:T(1,128)S(1)} %broadcast_in_dim.93.gauss_ref, bf16[2,640,640]{2,1,0:T(8,128)(2,1)S(1)} %copy-done), custom_call_target="tpu_custom_call" | custom-call | tf_op jit(solution)/shard_map/project/pallas_call | solution.py:372
  (8 shorter events, 0.0 us)
Async XLA Ops:
  0.6 22.2 %copy-start.11 = (pred[7,40]{1,0:T(8,128)(4,1)S(1)}, pred[7,40]{1,0:T(8,128)(4,1)}, u32[]{:S(2)}) copy-start(pred[7,40]{1,0:T(8,128)(4,1)} %constant.123.clone) | copy-start | bytes 844
  0.6 19.9 %copy-start.9 = (s32[32]{0:T(128)S(1)}, s32[32]{0:T(128)}, u32[]{:S(2)}) copy-start(s32[32]{0:T(128)} %low_ref.1) | copy-start | bytes 388
  0.7 19.8 %copy-start.8 = (s32[640]{0:T(1024)S(1)}, s32[640]{0:T(1024)}, u32[]{:S(2)}) copy-start(s32[640]{0:T(1024)} %points_ref.1) | copy-start | bytes 7684
  0.7 19.9 %copy-start.7 = (f32[2,1,1640]{2,1,0:T(1,128)S(1)}, f32[2,1,1640]{2,1,0:T(1,128)}, u32[]{:S(2)}) copy-start(f32[2,1,1640]{2,1,0:T(1,128)} %factor_ref.1) | copy-start | bytes 39364
  0.7 27.3 %copy-start.6 = (bf16[64,64]{1,0:T(8,128)(2,1)S(1)}, bf16[64,64]{1,0:T(8,128)(2,1)}, u32[]{:S(2)}) copy-start(bf16[64,64]{1,0:T(8,128)(2,1)} %param.15) | copy-start | bytes 24580
  3.1 24.9 %all-to-all-start.4 = ((bf16[16,8,128]{2,1,0:T(8,128)(2,1)}), bf16[16,8,128]{2,1,0:T(8,128)(2,1)S(1)}, u32[]{:S(2)}, u32[]{:S(2)}) async-start(bf16[16,8,128]{2,1,0:T(8,128)(2,1)} %legendre.1), calls=%async_computation.4 | async-start | bytes 65536 | tf_op jit(solution)/shard_map/all_to_all | solution.py:551
  28.0 67.7 %copy-start.10 = (f32[640]{0:T(1024)S(1)}, f32[640]{0:T(1024)}, u32[]{:S(2)}) copy-start(f32[640]{0:T(1024)} %param.14) | copy-start | bytes 7684
  28.0 75.0 %copy-start = (bf16[2,640,640]{2,1,0:T(8,128)(2,1)S(1)}, bf16[2,640,640]{2,1,0:T(8,128)(2,1)}, u32[]{:S(2)}) copy-start(bf16[2,640,640]{2,1,0:T(8,128)(2,1)} %leg_ref.1) | copy-start | bytes 4915204
  30.3 57.3 %copy-start.3 = (f32[2,40,8,128]{3,2,1,0:T(8,128)S(1)}, f32[2,40,8,128]{3,2,1,0:T(8,128)}, u32[]{:S(2)}) copy-start(f32[2,40,8,128]{3,2,1,0:T(8,128)} %get-tuple-element.44.coarse_ref) | copy-start | bytes 983044 | tf_op jit(solution)/shard_map/cond
  30.3 57.3 %copy-start.4 = (f32[2,40,8,128]{3,2,1,0:T(8,128)S(1)}, f32[2,40,8,128]{3,2,1,0:T(8,128)}, u32[]{:S(2)}) copy-start(f32[2,40,8,128]{3,2,1,0:T(8,128)} %get-tuple-element.45.fine_ref) | copy-start | bytes 983044 | tf_op jit(solution)/shard_map/cond
  30.3 57.3 %copy-start.5 = (bf16[7,128,128]{2,1,0:T(8,128)(2,1)S(1)}, bf16[7,128,128]{2,1,0:T(8,128)(2,1)}, u32[]{:S(2)}) copy-start(bf16[7,128,128]{2,1,0:T(8,128)(2,1)} %get-tuple-element.46.trig_ref) | copy-start | bytes 688132 | tf_op jit(solution)/shard_map/cond
  62.5 25.0 %all-to-all-start.1 = ((bf16[64,7,2,128]{3,2,1,0:T(2,128)(2,1)}), bf16[64,7,2,128]{3,2,1,0:T(2,128)(2,1)S(1)}, u32[]{:S(2)}, u32[]{:S(2)}) async-start(bf16[64,7,2,128]{3,2,1,0:T(2,128)(2,1)} %bitcast.24), calls=%async_computation.1 | async-start | bytes 458752 | tf_op jit(solution)/shard_map/cond/branch_1_fun/all_to_all | solution.py:556
  89.3 13.8 %all-to-all-start.5 = ((bf16[16,8,128]{2,1,0:T(8,128)(2,1)}), bf16[16,8,128]{2,1,0:T(8,128)(2,1)S(1)}, u32[]{:S(2)}, u32[]{:S(2)}) async-start(bf16[16,8,128]{2,1,0:T(8,128)(2,1)} %get-tuple-element.71), calls=%async_computation.5 | async-start | bytes 65536 | tf_op jit(solution)/shard_map/all_to_all | solution.py:567

commit v5 on v4

--- a/solution.py
+++ b/solution.py
@@ -26,12 +26,12 @@
     [3, 5, 17, 21, 27, 38],
 ]
 GROUPS = len(GROUP_ROWS)
-MOST = max(len(rows) for rows in GROUP_ROWS)
 SCALE = 2.0 / math.sqrt(40960.0)
 F32 = jnp.float32
 BF16 = jnp.bfloat16
 SMEM = pltpu.SMEM
 GRANT = 12 * 2**20
+PIECES = 5
 FULL_GRANT = 60 * 1024 * 2**10
 
 
@@ -138,7 +138,7 @@
             packed = jnp.where(mine, pltpu.roll(window, offset & (LANES - 1), axis=1), packed)
         slot_ref[0, group : group + 1, :] = which
         slot_ref[1, group : group + 1, :] = width
-        slot_ref[2, group : group + 1, :] = points - column
+        slot_ref[2, group : group + 1, :] = jnp.where(which < 0, 0, points - column)
         for h in range(2):
             pf_ref[h, group : group + 1, :] = packed[h : h + 1]
         points = jnp.broadcast_to(points.astype(F32), (LANES, LANES))
@@ -146,7 +146,7 @@
         trig_ref[group] = cos_turn(turn).astype(BF16)
 
 
-def synth_kernel(block_ref, coarse_ref, fine_ref, trig_ref, slot_ref, scale_ref, out_ref, a_ref, b_ref, lhs_ref, row_ref):
+def synth_kernel(block_ref, coarse_ref, fine_ref, trig_ref, slot_ref, scale_ref, out_ref, a_ref, b_ref, row_ref):
     even = (lane_iota((LANES, LANES)) & 1) == 0
     coeffs = jnp.transpose(block_ref[...].reshape(LANES, LANES).astype(F32))
     coeffs = jnp.where(scale_ref[...] > 0.0, coeffs, 0.0) * SCALE
@@ -154,33 +154,28 @@
     b_ref[...] = jnp.where(even, pltpu.roll(coeffs, LANES - 1, axis=1), coeffs)
     sector = lax.broadcasted_iota(jnp.int32, (NSECT, LANES), 0)
     for group in range(GROUPS):
-        used = 2 * NSECT * len(GROUP_ROWS[group])
+        which = slot_ref[0, group : group + 1, :]
+        total = None
         for i, row in enumerate(GROUP_ROWS[group]):
             cos = fine_ref[0, row]
             sin = fine_ref[1, row]
+            us = [coarse_ref[0, row, k : k + 1, :] for k in range(8)]
+            ws = [coarse_ref[1, row, k : k + 1, :] for k in range(8)]
+            tiles = []
             for h in range(2):
                 at = h * 64 + row
                 a = a_ref[at : at + 1, :]
                 b = b_ref[at : at + 1, :]
                 near = a * cos - b * sin
                 far = a * sin + b * cos
-                for block in range(0, 8, 2):
-                    pair = [
-                        coarse_ref[0, row, k : k + 1, :] * near + coarse_ref[1, row, k : k + 1, :] * far
-                        for k in (block, block + 1)
-                    ]
-                    place = (i * 2 + h) * NSECT + block * 8
-                    lhs_ref[place : place + 16, :] = jnp.concatenate(pair, axis=0).astype(BF16)
-        product = jnp.dot(lhs_ref[0:used, :], trig_ref[group], preferred_element_type=F32)
-        which = slot_ref[0, group : group + 1, :]
+                tiles += [us[k] * near + ws[k] * far for k in range(8)]
+            lhs = jnp.concatenate(tiles, axis=0).astype(BF16)
+            product = jnp.dot(lhs, trig_ref[group], preferred_element_type=F32)
+            total = product if total is None else jnp.where(which == i, product, total)
         valid = sector * slot_ref[1, group : group + 1, :] < slot_ref[2, group : group + 1, :]
-        which = jnp.where(valid, which, -1)
         for h in range(2):
-            total = jnp.zeros((NSECT, LANES), F32)
-            for i in range(len(GROUP_ROWS[group])):
-                place = (i * 2 + h) * NSECT
-                total = jnp.where(which == i, product[place : place + NSECT, :], total)
-            row_ref[pl.ds(2 * group + h, NSECT, stride=2 * GROUPS), :] = total
+            part = jnp.where(valid, total[h * NSECT : (h + 1) * NSECT, :], 0.0)
+            row_ref[pl.ds(2 * group + h, NSECT, stride=2 * GROUPS), :] = part
     out_ref[...] = row_ref[...].astype(BF16)
 
 
@@ -226,32 +221,31 @@
         out_ref[h] = wide_ref[:, 0 : ROWS * SECW].astype(BF16)
 
 
-def analysis_kernel(tend_ref, coarse_ref, fine_ref, trig_ref, slot_ref, scale_ref, out_ref, row_ref, lhs_ref, yu_ref, yw_ref):
+def analysis_kernel(tend_ref, coarse_ref, fine_ref, trig_ref, slot_ref, scale_ref, out_ref, row_ref, yu_ref, yw_ref):
     row_ref[...] = rows_of(tend_ref)
     yu_ref[...] = jnp.zeros((LANES, LANES), F32)
     yw_ref[...] = jnp.zeros((LANES, LANES), F32)
     for group in range(GROUPS):
         which = slot_ref[0, group : group + 1, :]
-        used = 2 * NSECT * len(GROUP_ROWS[group])
-        for h in range(2):
-            values = row_ref[pl.ds(2 * group + h, NSECT, stride=2 * GROUPS), :]
-            for i in range(len(GROUP_ROWS[group])):
-                place = (i * 2 + h) * NSECT
-                lhs_ref[place : place + NSECT, :] = jnp.where(which == i, values, 0.0).astype(BF16)
-        product = lax.dot_general(
-            lhs_ref[0:used, :], trig_ref[group], (((1,), (1,)), ((), ())), preferred_element_type=F32
+        values = jnp.concatenate(
+            [row_ref[pl.ds(2 * group + h, NSECT, stride=2 * GROUPS), :] for h in range(2)], axis=0
         )
         for i, row in enumerate(GROUP_ROWS[group]):
+            lhs = jnp.where(which == i, values, 0.0).astype(BF16)
+            product = lax.dot_general(
+                lhs, trig_ref[group], (((1,), (1,)), ((), ())), preferred_element_type=F32
+            )
             cos = fine_ref[0, row]
             sin = fine_ref[1, row]
+            us = [coarse_ref[0, row, k : k + 1, :] for k in range(8)]
+            ws = [coarse_ref[1, row, k : k + 1, :] for k in range(8)]
             for h in range(2):
                 near = jnp.zeros((8, LANES), F32)
                 far = jnp.zeros((8, LANES), F32)
-                for block in range(8):
-                    place = (i * 2 + h) * NSECT + block * 8
-                    sums = product[place : place + 8, :]
-                    near = near + sums * coarse_ref[0, row, block : block + 1, :]
-                    far = far + sums * coarse_ref[1, row, block : block + 1, :]
+                for k in range(8):
+                    sums = product[h * NSECT + 8 * k : h * NSECT + 8 * k + 8, :]
+                    near = near + sums * us[k]
+                    far = far + sums * ws[k]
                 at = h * 64 + row
                 yu_ref[at : at + 1, :] = jnp.sum(near * cos + far * sin, axis=0, keepdims=True)
                 yw_ref[at : at + 1, :] = jnp.sum(far * cos - near * sin, axis=0, keepdims=True)
@@ -272,17 +266,17 @@
 
 
 def legendre_kernel(low_hbm, spec_hbm, leg_hbm, out_ref, wide_ref, low_ref, spec_ref, leg_ref, sems):
-    low_copy = pltpu.make_async_copy(low_hbm, low_ref, sems.at[5])
+    low_copy = pltpu.make_async_copy(low_hbm, low_ref, sems.at[2 * PIECES + 1])
     low_copy.start()
-    spec_copy = pltpu.make_async_copy(spec_hbm, spec_ref, sems.at[4])
+    spec_copy = pltpu.make_async_copy(spec_hbm, spec_ref, sems.at[2 * PIECES])
     spec_copy.start()
-    half = NMAX // 2
+    piece = NMAX // PIECES
     leg_copies = []
     for p in range(2):
-        for part in range(2):
-            rows = pl.ds(part * half, half)
+        for part in range(PIECES):
+            rows = pl.ds(part * piece, piece)
             leg_copies.append(
-                pltpu.make_async_copy(leg_hbm.at[p, rows], leg_ref.at[p, rows], sems.at[2 * p + part])
+                pltpu.make_async_copy(leg_hbm.at[p, rows], leg_ref.at[p, rows], sems.at[PIECES * p + part])
             )
             leg_copies[-1].start()
     wide_ref[...] = jnp.zeros((16, 6 * LANES), F32)
@@ -302,8 +296,8 @@
         values.append(jnp.where((h == 1) & odd, -value, value).astype(BF16))
     found = []
     for p in range(2):
-        leg_copies[2 * p].wait()
-        leg_copies[2 * p + 1].wait()
+        for part in range(PIECES):
+            leg_copies[PIECES * p + part].wait()
         found.append(jnp.dot(values[p], leg_ref[p], preferred_element_type=F32))
     upper = line < 4
     wide_ref[0:8, 0:NMAX] = jnp.where(upper, found[0], pltpu.roll(found[1], 4, axis=0))
@@ -419,7 +413,6 @@
         [
             vmem((LANES, LANES), F32),
             vmem((LANES, LANES), F32),
-            vmem((2 * MOST * NSECT, LANES), BF16),
             vmem((LINES, LANES), F32),
         ],
         block, coarse, fine, trig, slots, scale,
@@ -456,7 +449,6 @@
         [whole()] * 6,
         [
             vmem((LINES, LANES), F32),
-            vmem((2 * MOST * NSECT, LANES), BF16),
             vmem((LANES, LANES), F32),
             vmem((LANES, LANES), F32),
         ],
@@ -475,7 +467,7 @@
             SMEM((32,), jnp.int32),
             vmem((2, 2, NMAX), BF16),
             vmem((2, NMAX, NMAX), BF16),
-            pltpu.SemaphoreType.DMA((6,)),
+            pltpu.SemaphoreType.DMA((2 * PIECES + 2,)),
         ],
         pair_low, spec, legendre,
         grant=FULL_GRANT,

time: 105 us -> 105 us (level)
  no operation moved by 1% of the time
where the time goes in v5:
time: 105 us; the launch traced here: 104 us
  blocking collectives  31.2 us (30%)
  starting transfers between devices  31.1 us (30%)
  waiting for transfers between devices  26.9 us (26%)
  Pallas kernels  12.7 us (12%)
  between operations  1.39 us (1%)
    all_to_all x1, blocking collectives, cross(): lax.all_to_all(x, 'sect', split_axis=0, concat_axis=0, tiled=True)  31.2 us
    all_to_all x1, starting transfers between devices, per_device(): lax.all_to_all(outgoing, WAVE, split_axis=0, concat_axis=0, tiled=True)  17.4 us
    all_to_all x1, waiting for transfers between devices, cross(): lax.all_to_all(x, 'sect', split_axis=0, concat_axis=0, tiled=True)  15.9 us
    pallas_call x7, Pallas kernels, run(): pl.pallas_call(kernel, out_shape=outs, in_specs=in_specs, out_specs=[whol...  12.7 us
    all_to_all x1, waiting for transfers between devices, per_device(): lax.all_to_all(analysis, WAVE, split_axis=0, concat_axis=0, tiled=True)  7.37 us
    all_to_all x1, starting transfers between devices, cross(): lax.all_to_all(x, 'sect', split_axis=0, concat_axis=0, tiled=True)  7.29 us
    all_to_all x1, starting transfers between devices, per_device(): lax.all_to_all(analysis, WAVE, split_axis=0, concat_axis=0, tiled=True)  6.38 us
    all_to_all x1, waiting for transfers between devices, per_device(): lax.all_to_all(outgoing, WAVE, split_axis=0, concat_axis=0, tiled=True)  3.63 us
  transfers between devices with their start and end apart: 3, of which 3 were waited for; matrix products, arithmetic and copies ran while one was open for 1% of the time, Pallas kernels for 4%

profile of v5, /device:TPU:1, one launch (start us, length us, event | category | flops | bytes accessed | tf_op | source)
XLA Modules:
  0.0 104.4 jit_solution(3869300711635745578)
XLA Ops:
  0.6 0.0 copy-start.11
  0.6 0.0 copy-start.9
  0.7 0.0 copy-start.8
  0.7 0.0 copy-start.7
  0.7 0.0 copy-start.6
  0.7 2.5 %legendre.1 = bf16[16,8,128]{2,1,0:T(8,128)(2,1)} custom-call(s32[32]{0:T(128)} %low_ref.1, bf16[2,2,640]{2,1,0:T(2,128)(2,1)} %bitcast.63, bf16[2,640,640]{2,1,0:T(8,128)(2,1)} %leg_ref.1), custom_call_target="tpu_custom_call" | custom-call | tf_op jit(solution)/shard_map/legendre/pallas_call | solution.py:366
  3.2 17.4 %all-to-all-start.4 = ((bf16[16,8,128]{2,1,0:T(8,128)(2,1)}), bf16[16,8,128]{2,1,0:T(8,128)(2,1)S(1)}, u32[]{:S(2)}, u32[]{:S(2)}) async-start(bf16[16,8,128]{2,1,0:T(8,128)(2,1)} %legendre.1), calls=%async_computation.4 | async-start | bytes 65536 | tf_op jit(solution)/shard_map/all_to_all | solution.py:543
  20.6 0.0 copy-done.8
  20.7 0.0 copy-done.9
  20.7 0.0 copy-done.7
  20.7 2.2 %tables.1 = (f32[2,40,8,128]{3,2,1,0:T(8,128)}, f32[2,40,8,128]{3,2,1,0:T(8,128)}, bf16[7,128,128]{2,1,0:T(8,128)(2,1)}, s32[3,7,128]{2,1,0:T(8,128)S(1)}, f32[2...) custom-call(s32[32]{0:T(128)S(1)} %copy-done.9, s32[640]{0:T(1024)S(1)} %copy-done.8, ...), custom_call_target="tpu_custom_call" | custom-call | tf_op jit(solution)/shard_map/tables/pallas_call | solution.py:366
  22.9 0.1 broadcast_in_dim.90
  23.0 0.0 copy-done.11
  23.0 0.2 select_reduce_fusion
  23.2 0.6 reduce_max.9
  24.5 3.6 %all-to-all-done.4 = bf16[16,8,128]{2,1,0:T(8,128)(2,1)S(1)} async-done(((bf16[16,8,128]{2,1,0:T(8,128)(2,1)}), bf16[16,8,128]{2,1,0:T(8,128)(2,1)S(1)}, u32[]{:S(2)}, u32[]{:S(2)}) %all-to-all-start.4) | async-done | bytes 32800 | tf_op jit(solution)/shard_map/all_to_all | solution.py:543
  28.1 0.0 copy-done.6
  28.1 61.3 %conditional.1 = (bf16[16,8,128]{2,1,0:T(8,128)(2,1)}, bf16[2,64,1,1640]{3,1,2,0:T(8,128)(2,1)}) conditional(s32[]{:T(128)} %convert_element_type.54, (s32[32]{0:T(128)S(1)}, s32[]{:T(128)}, s32[]{:T(128)}, s32[640]{0:T(1024)S(1)}, bf16[16,8,128]{2,1,0:T(8,128)(2,1)S(1)}, /*index=5*/bf16[64,64]{1,0:T(8,128)(2,1)S(1)}, ...), branch_computations={%region_2.5_spmd, %region_5.6_spmd} | conditional | flops 151992576 | bytes 32076354 | solution.py:558
  28.1 2.1 %synth.1 = bf16[896,128]{1,0:T(8,128)(2,1)S(1)} custom-call(bf16[16,8,128]{2,1,0:T(8,128)(2,1)S(1)} %get-tuple-element.43.block_ref, f32[2,40,8,128]{3,2,1,0:T(8,128)} %get-tuple-element.44.coarse_ref, f32[2,40,8,128]{3,2,1,0:T(8,128)} %get-tuple-element.45.fine_ref, bf16[7,128,128]{2,1,0:T(8,128)(2,1)} %get-tuple-element.46.trig_ref, ...), custom_call_target="tpu_custom_call" | custom-call | tf_op jit(solution)/shard_map/cond/branch_1_fun/synth/pallas_call | solution.py:366
  30.3 0.0 copy-start.3
  30.3 0.0 copy-start.4
  30.3 31.2 %all_to_all.26 = bf16[64,7,2,128]{3,2,1,0:T(2,128)(2,1)S(1)} all-to-all(bf16[64,7,2,128]{3,2,1,0:T(2,128)(2,1)S(1)} %bitcast.53), channel_id=1, replica_groups=mesh['wave_0'=8,'wave_1'=2,'sect'=64] {'sect'}, dimensions={0} | all-to-all | bytes 458752 | tf_op jit(solution)/shard_map/cond/branch_1_fun/all_to_all | solution.py:548
  61.5 1.0 tendency.1
  62.5 7.3 %all-to-all-start.1 = ((bf16[64,7,2,128]{3,2,1,0:T(2,128)(2,1)}), bf16[64,7,2,128]{3,2,1,0:T(2,128)(2,1)S(1)}, u32[]{:S(2)}, u32[]{:S(2)}) async-start(bf16[64,7,2,128]{3,2,1,0:T(2,128)(2,1)} %bitcast.24), calls=%async_computation.1 | async-start | bytes 458752 | tf_op jit(solution)/shard_map/cond/branch_1_fun/all_to_all | solution.py:548
  69.8 1.9 %expand.1 = bf16[2,64,1640]{2,1,0:T(8,128)(2,1)} custom-call(s32[640]{0:T(1024)S(1)} %get-tuple-element.51.points_ref, bf16[896,128]{1,0:T(8,128)(2,1)S(1)} %bitcast.51), custom_call_target="tpu_custom_call" | custom-call | tf_op jit(solution)/shard_map/cond/branch_1_fun/expand/pallas_call | solution.py:366
  71.7 15.9 %all-to-all-done.1 = bf16[64,7,2,128]{3,2,1,0:T(2,128)(2,1)S(1)} async-done(((bf16[64,7,2,128]{3,2,1,0:T(2,128)(2,1)}), bf16[64,7,2,128]{3,2,1,0:T(2,128)(2,1)S(1)}, u32[]{:S(2)}, u32[]{:S(2)}) %all-to-all-start.1) | async-done | bytes 229408 | tf_op jit(solution)/shard_map/cond/branch_1_fun/all_to_all | solution.py:548
  87.5 0.0 copy-done.5
  87.6 1.8 %analysis.1 = bf16[16,8,128]{2,1,0:T(8,128)(2,1)} custom-call(bf16[896,128]{1,0:T(8,128)(2,1)S(1)} %bitcast.52, f32[2,40,8,128]{3,2,1,0:T(8,128)S(1)} %copy-done.3, f32[2,40,8,128]{3,2,1,0:T(8,128)S(1)} %copy-done.4, bf16[7,128,128]{2,1,0:T(8,128)(2,1)S(1)} %copy-done.5, s32[3,7,128]{2,1,0:T(8,128)S(1)} %get-tuple-element.47.slot_ref, ...), custom_call_target="tpu_custom_call" | custom-call | tf_op jit(solution)/shard_map/cond/branch_1_fun/analysis/pallas_call | solution.py:366
  89.4 6.4 %all-to-all-start.5 = ((bf16[16,8,128]{2,1,0:T(8,128)(2,1)}), bf16[16,8,128]{2,1,0:T(8,128)(2,1)S(1)}, u32[]{:S(2)}, u32[]{:S(2)}) async-start(bf16[16,8,128]{2,1,0:T(8,128)(2,1)} %get-tuple-element.71), calls=%async_computation.5 | async-start | bytes 65536 | tf_op jit(solution)/shard_map/all_to_all | solution.py:559
  95.8 0.0 copy-done.10
  95.8 7.4 %all-to-all-done.5.back_ref = bf16[16,8,128]{2,1,0:T(8,128)(2,1)S(1)} async-done(((bf16[16,8,128]{2,1,0:T(8,128)(2,1)}), bf16[16,8,128]{2,1,0:T(8,128)(2,1)S(1)}, u32[]{:S(2)}, u32[]{:S(2)}) %all-to-all-start.5) | async-done | bytes 32800 | tf_op jit(solution)/shard_map/all_to_all | solution.py:559
  103.2 1.2 %project.1 = f32[4,1,640]{2,1,0:T(1,128)} custom-call(s32[2,640]{1,0:T(2,128)S(1)} %get-tuple-element.70.pick_ref, bf16[16,8,128]{2,1,0:T(8,128)(2,1)S(1)} %all-to-all-done.5.back_ref, f32[1,640]{1,0:T(1,128)S(1)} %broadcast_in_dim.93.gauss_ref, bf16[2,640,640]{2,1,0:T(8,128)(2,1)S(1)} %copy-done), custom_call_target="tpu_custom_call" | custom-call | tf_op jit(solution)/shard_map/project/pallas_call | solution.py:366
  (8 shorter events, 0.0 us)
Async XLA Ops:
  0.6 22.4 %copy-start.11 = (pred[7,40]{1,0:T(8,128)(4,1)S(1)}, pred[7,40]{1,0:T(8,128)(4,1)}, u32[]{:S(2)}) copy-start(pred[7,40]{1,0:T(8,128)(4,1)} %constant.123.clone) | copy-start | bytes 844
  0.6 20.0 %copy-start.9 = (s32[32]{0:T(128)S(1)}, s32[32]{0:T(128)}, u32[]{:S(2)}) copy-start(s32[32]{0:T(128)} %low_ref.1) | copy-start | bytes 388
  0.7 20.0 %copy-start.8 = (s32[640]{0:T(1024)S(1)}, s32[640]{0:T(1024)}, u32[]{:S(2)}) copy-start(s32[640]{0:T(1024)} %points_ref.1) | copy-start | bytes 7684
  0.7 20.0 %copy-start.7 = (f32[2,1,1640]{2,1,0:T(1,128)S(1)}, f32[2,1,1640]{2,1,0:T(1,128)}, u32[]{:S(2)}) copy-start(f32[2,1,1640]{2,1,0:T(1,128)} %factor_ref.1) | copy-start | bytes 39364
  0.7 27.5 %copy-start.6 = (bf16[64,64]{1,0:T(8,128)(2,1)S(1)}, bf16[64,64]{1,0:T(8,128)(2,1)}, u32[]{:S(2)}) copy-start(bf16[64,64]{1,0:T(8,128)(2,1)} %param.15) | copy-start | bytes 24580
  3.2 24.9 %all-to-all-start.4 = ((bf16[16,8,128]{2,1,0:T(8,128)(2,1)}), bf16[16,8,128]{2,1,0:T(8,128)(2,1)S(1)}, u32[]{:S(2)}, u32[]{:S(2)}) async-start(bf16[16,8,128]{2,1,0:T(8,128)(2,1)} %legendre.1), calls=%async_computation.4 | async-start | bytes 65536 | tf_op jit(solution)/shard_map/all_to_all | solution.py:543
  28.1 67.7 %copy-start.10 = (f32[640]{0:T(1024)S(1)}, f32[640]{0:T(1024)}, u32[]{:S(2)}) copy-start(f32[640]{0:T(1024)} %param.14) | copy-start | bytes 7684
  28.1 75.0 %copy-start = (bf16[2,640,640]{2,1,0:T(8,128)(2,1)S(1)}, bf16[2,640,640]{2,1,0:T(8,128)(2,1)}, u32[]{:S(2)}) copy-start(bf16[2,640,640]{2,1,0:T(8,128)(2,1)} %leg_ref.1) | copy-start | bytes 4915204
  30.3 57.3 %copy-start.3 = (f32[2,40,8,128]{3,2,1,0:T(8,128)S(1)}, f32[2,40,8,128]{3,2,1,0:T(8,128)}, u32[]{:S(2)}) copy-start(f32[2,40,8,128]{3,2,1,0:T(8,128)} %get-tuple-element.44.coarse_ref) | copy-start | bytes 983044 | tf_op jit(solution)/shard_map/cond
  30.3 57.3 %copy-start.4 = (f32[2,40,8,128]{3,2,1,0:T(8,128)S(1)}, f32[2,40,8,128]{3,2,1,0:T(8,128)}, u32[]{:S(2)}) copy-start(f32[2,40,8,128]{3,2,1,0:T(8,128)} %get-tuple-element.45.fine_ref) | copy-start | bytes 983044 | tf_op jit(solution)/shard_map/cond
  30.3 57.3 %copy-start.5 = (bf16[7,128,128]{2,1,0:T(8,128)(2,1)S(1)}, bf16[7,128,128]{2,1,0:T(8,128)(2,1)}, u32[]{:S(2)}) copy-start(bf16[7,128,128]{2,1,0:T(8,128)(2,1)} %get-tuple-element.46.trig_ref) | copy-start | bytes 688132 | tf_op jit(solution)/shard_map/cond
  62.5 25.0 %all-to-all-start.1 = ((bf16[64,7,2,128]{3,2,1,0:T(2,128)(2,1)}), bf16[64,7,2,128]{3,2,1,0:T(2,128)(2,1)S(1)}, u32[]{:S(2)}, u32[]{:S(2)}) async-start(bf16[64,7,2,128]{3,2,1,0:T(2,128)(2,1)} %bitcast.24), calls=%async_computation.1 | async-start | bytes 458752 | tf_op jit(solution)/shard_map/cond/branch_1_fun/all_to_all | solution.py:548
  89.4 13.8 %all-to-all-start.5 = ((bf16[16,8,128]{2,1,0:T(8,128)(2,1)}), bf16[16,8,128]{2,1,0:T(8,128)(2,1)S(1)}, u32[]{:S(2)}, u32[]{:S(2)}) async-start(bf16[16,8,128]{2,1,0:T(8,128)(2,1)} %get-tuple-element.71), calls=%async_computation.5 | async-start | bytes 65536 | tf_op jit(solution)/shard_map/all_to_all | solution.py:559
